TPU v7x, 512 devices: a whole 4x4x16 slice. The times are simulated.
512 devices in a mesh: light: 16 (over y, x), view: 32 (over z, core).
Axes of the slice: x: 4, y: 4, z: 16, core: 2. Of those that a mesh axis runs over, the one named last changes fastest.
Arguments:
- density: float32 [128, 256, 2048], P('light', 'view'), may hold values from 0.1 to 2
- albedo: bfloat16 [3, 128, 256, 2048], P(None, 'light', 'view'), may hold values from 0.099609375 to 1
- light_color: float32 [8, 3], replicated, may hold values from 0.5 to 1.5
- light_shift: int32 [8], replicated, may hold values from -1 to 1
- view_flip: int32 [128], P('light'), may hold values 0 or 1
Outputs:
- images: float32 [8, 4, 262144], P(None, None, ('light', 'view'))
Inputs may be any that keep to these rules, and one draw needn't show every extreme that they name: `light_shift`: every light steps sideways by at most one cell per slice. `view_flip`: 0 means lower view indices lie in front, 1 means higher ones do.
All inputs are finite; a program needn't handle non-finite values. No bound on the sum of `view_flip` on one device may be relied on, other than what follows from the above.
Results may differ from a plain program's by a relative error of at most 0.0003.
Values sent between devices are 32-bit elements; how exact they have to be, the bound alone decides.
No kernel may reach another device: no remote copies, remote signals or barrier semaphores. Data moves between devices by JAX's collectives and lax.ppermute only.
A program may use at most 64 MiB of HBM per device.

v0:
```python
import jax
import jax.numpy as jnp
from jax import lax
from jax.sharding import PartitionSpec as P

LIGHTS = 8
FRONT = 4


LIGHT_DEPTH = 1.5
VIEW_DEPTH = 2.0


def partner(value, axis, bit):
    mask = 2**bit
    pairs = [(source, source ^ mask) for source in range(lax.axis_size(axis))]
    return lax.ppermute(value, axis, pairs)


def shifted(value, axis, steps):
    count = lax.axis_size(axis)
    leading, last = (max(0, -steps), min(count, count - steps))
    return lax.ppermute(value, axis, [(source, source + steps) for source in range(leading, last)])


def move_cells(planes, amount):
    columns = planes.shape[-1]
    filler = jnp.ones(planes.shape[:-1] + (abs(amount),), planes.dtype)
    if amount > 0:
        return jnp.concatenate([filler, planes[..., : columns - amount]], axis=-1)
    return jnp.concatenate([planes[..., -amount:], filler], axis=-1)


def slide_cells(planes, lateral, amount):
    forward = move_cells(planes, amount)
    backward = move_cells(planes, -amount)
    return jnp.where(lateral == 1, forward, jnp.where(lateral == -1, backward, planes))


def binary_swap(images, flip_pixels):
    view_count = lax.axis_size("view")
    view_index = lax.axis_index("view")
    piece_size = images.shape[-1] // view_count
    leading = images.shape[:-1]
    current = images
    current_flip = flip_pixels
    for bit_index in range(view_count.bit_length() - 1):
        blocks = current.shape[-1] // piece_size
        split_view = current.reshape(leading + (blocks // 2, 2 * piece_size))
        split_flip = current_flip.reshape((blocks // 2, 2 * piece_size))
        lower_half = split_view[..., :piece_size]
        upper_half = split_view[..., piece_size:]
        own_bit = view_index >> bit_index & 1
        kept_half = jnp.where(own_bit == 1, upper_half, lower_half)
        outgoing = jnp.where(own_bit == 1, lower_half, upper_half)
        kept_flip = jnp.where(own_bit == 1, split_flip[:, piece_size:], split_flip[:, :piece_size])
        received = partner(outgoing, "view", bit_index)
        partner_front = (own_bit == 1) != (kept_flip == 1)
        front_half = jnp.where(partner_front, received, kept_half)
        back_half = jnp.where(partner_front, kept_half, received)
        current = (front_half + (1.0 - front_half[:, 3:4]) * back_half).reshape(leading + (-1,))
        current_flip = kept_flip.reshape(-1)
    return current


def local(density, albedo, light_color, light_shift, view_flip):
    slices, cells, columns = density.shape
    light_count = lax.axis_size("light")
    view_count = lax.axis_size("view")
    light_step = LIGHT_DEPTH / (slices * light_count)
    view_step = VIEW_DEPTH / (cells * view_count)
    flipped = view_flip[:, None, None]
    flip_pixels = jnp.repeat(view_flip, columns)
    light_index = lax.axis_index("light")
    depth_view = density * view_step
    running = jnp.cumsum(depth_view, axis=1)
    column_total = running[:, -1, :]
    ahead_depth = jnp.where(flipped == 1, column_total[:, None, :] - running, running - depth_view)
    weights = jnp.exp(-ahead_depth) * (1.0 - jnp.exp(-depth_view))
    opacity = 1.0 - jnp.exp(-column_total)
    extinction = jnp.exp(-density * light_step)
    batches = []
    for batch_index in range(LIGHTS // FRONT):
        first = batch_index * FRONT
        lateral = light_shift[first : first + FRONT][:, None, None]
        light_tint = light_color[first : first + FRONT]
        partial_value = []
        exit_part = jnp.ones((FRONT, cells, columns), jnp.float32)
        for slice_index in range(slices):
            partial_value.append(exit_part)
            exit_part = slide_cells(exit_part * extinction[slice_index][None], lateral, 1)

        def hop_once(hop_index, carried):
            entering_now, leaving = carried
            incoming = shifted(leaving, "light", 1)
            entering_now = jnp.where(light_index == hop_index + 1, incoming, entering_now)
            return (entering_now, slide_cells(entering_now, lateral, slices) * exit_part)

        entering, _ = lax.fori_loop(
            0, light_count - 1, hop_once, (jnp.ones_like(exit_part), exit_part)
        )
        colour_rows = []
        current = entering
        for slice_index in range(slices):
            lit_cells = current * partial_value[slice_index] * weights[slice_index][None]
            reflect = albedo[:, slice_index].astype(jnp.float32)
            colour = jnp.sum(reflect[None] * lit_cells[:, None], axis=2)
            colour = colour * light_tint[:, :, None]
            alpha_row = jnp.broadcast_to(opacity[slice_index][None, None, :], (FRONT, 1, columns))
            colour = jnp.concatenate([colour, alpha_row], axis=1)
            colour_rows.append(colour)
            current = slide_cells(current, lateral, 1)
        images = jnp.concatenate(colour_rows, axis=2)
        batches.append(images)
    stacked = jnp.concatenate(batches, axis=0)
    return binary_swap(stacked, flip_pixels)


def solution(mesh):
    return jax.shard_map(
        local,
        mesh=mesh,
        in_specs=(P("light", "view", None), P(None, "light", "view", None), P(), P(), P("light")),
        out_specs=P(None, None, ("light", "view")),
        check_vma=False,
    )
```

profile of v0, /device:TPU:16, one launch (start us, length us, event | category | flops | bytes accessed | tf_op | source)
XLA Modules:
  0.0 484.4 jit_solution(1350725661504189171)
XLA Ops:
  18.3 184.7 %while.33 = (s32[]{:T(128)}, f32[4,8,2048]{2,1,0:T(8,128)S(1)}, f32[4,8,2048]{2,1,0:T(8,128)}, s32[]{:T(128)}, s32[4,1,1]{0,2,1:T(1,128)S(1)}, /*index=5*/f32[4,8,2048]{2,1,0:T(8,128)S(1)}, s32[]{:T(128)}, s32[]{:T(128)}) while((s32[]{:T(128)}, f32[4,8,2048]{2,1,0:T(8,128)S(1)}, f32[4,8,2048]{2,1,0:T(8,128)}, s32[]{:T(128)}, ...), condition=%wide.region_12.13_spmd.clone, body=%wide.region_11.12_spmd.clone.sunk | while | flops 327692 | bytes 4188345 | solution.py:99
  18.3 3.4 collective-permute-start.1
  21.7 8.8 %collective-permute-done.1 = f32[4,8,2048]{2,1,0:T(8,128)S(1)} collective-permute-done((f32[4,8,2048]{2,1,0:T(8,128)}, f32[4,8,2048]{2,1,0:T(8,128)S(1)}, u32[]{:S(2)}, u32[]{:S(2)}) %collective-permute-start.1) | collective-permute-done | bytes 262176 | tf_op jit(solution)/shard_map/while/body/eval_jaxpr/ppermute | solution.py:23
  33.5 9.5 %collective-permute-done.1 = f32[4,8,2048]{2,1,0:T(8,128)S(1)} collective-permute-done((f32[4,8,2048]{2,1,0:T(8,128)}, f32[4,8,2048]{2,1,0:T(8,128)S(1)}, u32[]{:S(2)}, u32[]{:S(2)}) %collective-permute-start.1) | collective-permute-done | bytes 262176 | tf_op jit(solution)/shard_map/while/body/eval_jaxpr/ppermute | solution.py:23
  46.0 8.6 %collective-permute-done.1 = f32[4,8,2048]{2,1,0:T(8,128)S(1)} collective-permute-done((f32[4,8,2048]{2,1,0:T(8,128)}, f32[4,8,2048]{2,1,0:T(8,128)S(1)}, u32[]{:S(2)}, u32[]{:S(2)}) %collective-permute-start.1) | collective-permute-done | bytes 262176 | tf_op jit(solution)/shard_map/while/body/eval_jaxpr/ppermute | solution.py:23
  57.6 8.6 %collective-permute-done.1 = f32[4,8,2048]{2,1,0:T(8,128)S(1)} collective-permute-done((f32[4,8,2048]{2,1,0:T(8,128)}, f32[4,8,2048]{2,1,0:T(8,128)S(1)}, u32[]{:S(2)}, u32[]{:S(2)}) %collective-permute-start.1) | collective-permute-done | bytes 262176 | tf_op jit(solution)/shard_map/while/body/eval_jaxpr/ppermute | solution.py:23
  69.2 8.6 %collective-permute-done.1 = f32[4,8,2048]{2,1,0:T(8,128)S(1)} collective-permute-done((f32[4,8,2048]{2,1,0:T(8,128)}, f32[4,8,2048]{2,1,0:T(8,128)S(1)}, u32[]{:S(2)}, u32[]{:S(2)}) %collective-permute-start.1) | collective-permute-done | bytes 262176 | tf_op jit(solution)/shard_map/while/body/eval_jaxpr/ppermute | solution.py:23
  80.9 8.6 %collective-permute-done.1 = f32[4,8,2048]{2,1,0:T(8,128)S(1)} collective-permute-done((f32[4,8,2048]{2,1,0:T(8,128)}, f32[4,8,2048]{2,1,0:T(8,128)S(1)}, u32[]{:S(2)}, u32[]{:S(2)}) %collective-permute-start.1) | collective-permute-done | bytes 262176 | tf_op jit(solution)/shard_map/while/body/eval_jaxpr/ppermute | solution.py:23
  92.5 8.6 %collective-permute-done.1 = f32[4,8,2048]{2,1,0:T(8,128)S(1)} collective-permute-done((f32[4,8,2048]{2,1,0:T(8,128)}, f32[4,8,2048]{2,1,0:T(8,128)S(1)}, u32[]{:S(2)}, u32[]{:S(2)}) %collective-permute-start.1) | collective-permute-done | bytes 262176 | tf_op jit(solution)/shard_map/while/body/eval_jaxpr/ppermute | solution.py:23
  104.2 9.5 %collective-permute-done.1 = f32[4,8,2048]{2,1,0:T(8,128)S(1)} collective-permute-done((f32[4,8,2048]{2,1,0:T(8,128)}, f32[4,8,2048]{2,1,0:T(8,128)S(1)}, u32[]{:S(2)}, u32[]{:S(2)}) %collective-permute-start.1) | collective-permute-done | bytes 262176 | tf_op jit(solution)/shard_map/while/body/eval_jaxpr/ppermute | solution.py:23
  116.7 10.7 %collective-permute-done.1 = f32[4,8,2048]{2,1,0:T(8,128)S(1)} collective-permute-done((f32[4,8,2048]{2,1,0:T(8,128)}, f32[4,8,2048]{2,1,0:T(8,128)S(1)}, u32[]{:S(2)}, u32[]{:S(2)}) %collective-permute-start.1) | collective-permute-done | bytes 262176 | tf_op jit(solution)/shard_map/while/body/eval_jaxpr/ppermute | solution.py:23
  130.4 11.0 %collective-permute-done.1 = f32[4,8,2048]{2,1,0:T(8,128)S(1)} collective-permute-done((f32[4,8,2048]{2,1,0:T(8,128)}, f32[4,8,2048]{2,1,0:T(8,128)S(1)}, u32[]{:S(2)}, u32[]{:S(2)}) %collective-permute-start.1) | collective-permute-done | bytes 262176 | tf_op jit(solution)/shard_map/while/body/eval_jaxpr/ppermute | solution.py:23
  144.5 10.2 %collective-permute-done.1 = f32[4,8,2048]{2,1,0:T(8,128)S(1)} collective-permute-done((f32[4,8,2048]{2,1,0:T(8,128)}, f32[4,8,2048]{2,1,0:T(8,128)S(1)}, u32[]{:S(2)}, u32[]{:S(2)}) %collective-permute-start.1) | collective-permute-done | bytes 262176 | tf_op jit(solution)/shard_map/while/body/eval_jaxpr/ppermute | solution.py:23
  157.7 9.3 %collective-permute-done.1 = f32[4,8,2048]{2,1,0:T(8,128)S(1)} collective-permute-done((f32[4,8,2048]{2,1,0:T(8,128)}, f32[4,8,2048]{2,1,0:T(8,128)S(1)}, u32[]{:S(2)}, u32[]{:S(2)}) %collective-permute-start.1) | collective-permute-done | bytes 262176 | tf_op jit(solution)/shard_map/while/body/eval_jaxpr/ppermute | solution.py:23
  170.0 8.6 %collective-permute-done.1 = f32[4,8,2048]{2,1,0:T(8,128)S(1)} collective-permute-done((f32[4,8,2048]{2,1,0:T(8,128)}, f32[4,8,2048]{2,1,0:T(8,128)S(1)}, u32[]{:S(2)}, u32[]{:S(2)}) %collective-permute-start.1) | collective-permute-done | bytes 262176 | tf_op jit(solution)/shard_map/while/body/eval_jaxpr/ppermute | solution.py:23
  181.6 8.6 %collective-permute-done.1 = f32[4,8,2048]{2,1,0:T(8,128)S(1)} collective-permute-done((f32[4,8,2048]{2,1,0:T(8,128)}, f32[4,8,2048]{2,1,0:T(8,128)S(1)}, u32[]{:S(2)}, u32[]{:S(2)}) %collective-permute-start.1) | collective-permute-done | bytes 262176 | tf_op jit(solution)/shard_map/while/body/eval_jaxpr/ppermute | solution.py:23
  193.3 8.6 %collective-permute-done.1 = f32[4,8,2048]{2,1,0:T(8,128)S(1)} collective-permute-done((f32[4,8,2048]{2,1,0:T(8,128)}, f32[4,8,2048]{2,1,0:T(8,128)S(1)}, u32[]{:S(2)}, u32[]{:S(2)}) %collective-permute-start.1) | collective-permute-done | bytes 262176 | tf_op jit(solution)/shard_map/while/body/eval_jaxpr/ppermute | solution.py:23
  203.9 173.4 %while.32 = (s32[]{:T(128)}, f32[4,8,2048]{2,1,0:T(8,128)S(1)}, f32[4,8,2048]{2,1,0:T(8,128)S(1)}, s32[]{:T(128)}, s32[4,1,1]{0,2,1:T(1,128)}, /*index=5*/f32[4,8,2048]{2,1,0:T(8,128)S(1)}, s32[]{:T(128)}, s32[]{:T(128)}) while((s32[]{:T(128)}, f32[4,8,2048]{2,1,0:T(8,128)S(1)}, f32[4,8,2048]{2,1,0:T(8,128)S(1)}, s32[]{:T(128)}, ...), condition=%wide.region_1.2_spmd.clone, body=%wide.region_0.0_spmd.clone.sunk | while | flops 327692 | bytes 4188345 | solution.py:99
  203.9 2.1 collective-permute-start
  206.7 8.2 %collective-permute-done = f32[4,8,2048]{2,1,0:T(8,128)S(1)} collective-permute-done((f32[4,8,2048]{2,1,0:T(8,128)S(1)}, f32[4,8,2048]{2,1,0:T(8,128)S(1)}, u32[]{:S(2)}, u32[]{:S(2)}) %collective-permute-start) | collective-permute-done | bytes 262176 | tf_op jit(solution)/shard_map/while/body/eval_jaxpr/ppermute | solution.py:23
  215.3 1.9 collective-permute-start
  217.9 9.4 %collective-permute-done = f32[4,8,2048]{2,1,0:T(8,128)S(1)} collective-permute-done((f32[4,8,2048]{2,1,0:T(8,128)S(1)}, f32[4,8,2048]{2,1,0:T(8,128)S(1)}, u32[]{:S(2)}, u32[]{:S(2)}) %collective-permute-start) | collective-permute-done | bytes 262176 | tf_op jit(solution)/shard_map/while/body/eval_jaxpr/ppermute | solution.py:23
  230.3 10.5 %collective-permute-done = f32[4,8,2048]{2,1,0:T(8,128)S(1)} collective-permute-done((f32[4,8,2048]{2,1,0:T(8,128)S(1)}, f32[4,8,2048]{2,1,0:T(8,128)S(1)}, u32[]{:S(2)}, u32[]{:S(2)}) %collective-permute-start) | collective-permute-done | bytes 262176 | tf_op jit(solution)/shard_map/while/body/eval_jaxpr/ppermute | solution.py:23
  243.8 9.7 %collective-permute-done = f32[4,8,2048]{2,1,0:T(8,128)S(1)} collective-permute-done((f32[4,8,2048]{2,1,0:T(8,128)S(1)}, f32[4,8,2048]{2,1,0:T(8,128)S(1)}, u32[]{:S(2)}, u32[]{:S(2)}) %collective-permute-start) | collective-permute-done | bytes 262176 | tf_op jit(solution)/shard_map/while/body/eval_jaxpr/ppermute | solution.py:23
  253.9 1.9 collective-permute-start
  256.6 8.8 %collective-permute-done = f32[4,8,2048]{2,1,0:T(8,128)S(1)} collective-permute-done((f32[4,8,2048]{2,1,0:T(8,128)S(1)}, f32[4,8,2048]{2,1,0:T(8,128)S(1)}, u32[]{:S(2)}, u32[]{:S(2)}) %collective-permute-start) | collective-permute-done | bytes 262176 | tf_op jit(solution)/shard_map/while/body/eval_jaxpr/ppermute | solution.py:23
  268.4 8.0 %collective-permute-done = f32[4,8,2048]{2,1,0:T(8,128)S(1)} collective-permute-done((f32[4,8,2048]{2,1,0:T(8,128)S(1)}, f32[4,8,2048]{2,1,0:T(8,128)S(1)}, u32[]{:S(2)}, u32[]{:S(2)}) %collective-permute-start) | collective-permute-done | bytes 262176 | tf_op jit(solution)/shard_map/while/body/eval_jaxpr/ppermute | solution.py:23
  279.4 7.7 %collective-permute-done = f32[4,8,2048]{2,1,0:T(8,128)S(1)} collective-permute-done((f32[4,8,2048]{2,1,0:T(8,128)S(1)}, f32[4,8,2048]{2,1,0:T(8,128)S(1)}, u32[]{:S(2)}, u32[]{:S(2)}) %collective-permute-start) | collective-permute-done | bytes 262176 | tf_op jit(solution)/shard_map/while/body/eval_jaxpr/ppermute | solution.py:23
  290.2 7.7 %collective-permute-done = f32[4,8,2048]{2,1,0:T(8,128)S(1)} collective-permute-done((f32[4,8,2048]{2,1,0:T(8,128)S(1)}, f32[4,8,2048]{2,1,0:T(8,128)S(1)}, u32[]{:S(2)}, u32[]{:S(2)}) %collective-permute-start) | collective-permute-done | bytes 262176 | tf_op jit(solution)/shard_map/while/body/eval_jaxpr/ppermute | solution.py:23
  301.0 7.7 %collective-permute-done = f32[4,8,2048]{2,1,0:T(8,128)S(1)} collective-permute-done((f32[4,8,2048]{2,1,0:T(8,128)S(1)}, f32[4,8,2048]{2,1,0:T(8,128)S(1)}, u32[]{:S(2)}, u32[]{:S(2)}) %collective-permute-start) | collective-permute-done | bytes 262176 | tf_op jit(solution)/shard_map/while/body/eval_jaxpr/ppermute | solution.py:23
  311.7 7.8 %collective-permute-done = f32[4,8,2048]{2,1,0:T(8,128)S(1)} collective-permute-done((f32[4,8,2048]{2,1,0:T(8,128)S(1)}, f32[4,8,2048]{2,1,0:T(8,128)S(1)}, u32[]{:S(2)}, u32[]{:S(2)}) %collective-permute-start) | collective-permute-done | bytes 262176 | tf_op jit(solution)/shard_map/while/body/eval_jaxpr/ppermute | solution.py:23
  319.9 1.9 collective-permute-start
  322.6 8.9 %collective-permute-done = f32[4,8,2048]{2,1,0:T(8,128)S(1)} collective-permute-done((f32[4,8,2048]{2,1,0:T(8,128)S(1)}, f32[4,8,2048]{2,1,0:T(8,128)S(1)}, u32[]{:S(2)}, u32[]{:S(2)}) %collective-permute-start) | collective-permute-done | bytes 262176 | tf_op jit(solution)/shard_map/while/body/eval_jaxpr/ppermute | solution.py:23
  334.5 10.1 %collective-permute-done = f32[4,8,2048]{2,1,0:T(8,128)S(1)} collective-permute-done((f32[4,8,2048]{2,1,0:T(8,128)S(1)}, f32[4,8,2048]{2,1,0:T(8,128)S(1)}, u32[]{:S(2)}, u32[]{:S(2)}) %collective-permute-start) | collective-permute-done | bytes 262176 | tf_op jit(solution)/shard_map/while/body/eval_jaxpr/ppermute | solution.py:23
  347.6 7.7 %collective-permute-done = f32[4,8,2048]{2,1,0:T(8,128)S(1)} collective-permute-done((f32[4,8,2048]{2,1,0:T(8,128)S(1)}, f32[4,8,2048]{2,1,0:T(8,128)S(1)}, u32[]{:S(2)}, u32[]{:S(2)}) %collective-permute-start) | collective-permute-done | bytes 262176 | tf_op jit(solution)/shard_map/while/body/eval_jaxpr/ppermute | solution.py:23
  358.4 7.7 %collective-permute-done = f32[4,8,2048]{2,1,0:T(8,128)S(1)} collective-permute-done((f32[4,8,2048]{2,1,0:T(8,128)S(1)}, f32[4,8,2048]{2,1,0:T(8,128)S(1)}, u32[]{:S(2)}, u32[]{:S(2)}) %collective-permute-start) | collective-permute-done | bytes 262176 | tf_op jit(solution)/shard_map/while/body/eval_jaxpr/ppermute | solution.py:23
  369.2 7.7 %collective-permute-done = f32[4,8,2048]{2,1,0:T(8,128)S(1)} collective-permute-done((f32[4,8,2048]{2,1,0:T(8,128)S(1)}, f32[4,8,2048]{2,1,0:T(8,128)S(1)}, u32[]{:S(2)}, u32[]{:S(2)}) %collective-permute-start) | collective-permute-done | bytes 262176 | tf_op jit(solution)/shard_map/while/body/eval_jaxpr/ppermute | solution.py:23
  378.4 2.1 fusion.6
  401.3 2.9 reshape.155
  407.5 2.7 collective-permute-done.2
  413.7 3.8 collective-permute-start.3
  417.7 12.0 %collective-permute-done.3 = f32[8,4,8,512]{3,2,1,0:T(8,128)S(1)} collective-permute-done((f32[8,4,8,512]{3,2,1,0:T(8,128)S(1)}, f32[8,4,8,512]{3,2,1,0:T(8,128)S(1)}, u32[]{:S(2)}, u32[]{:S(2)}) %collective-permute-start.3) | collective-permute-done | bytes 524320 | tf_op jit(solution)/shard_map/ppermute | solution.py:17
  430.5 5.2 %collective-permute-start.4 = (f32[8,4,4,512]{3,2,1,0:T(4,128)S(1)}, f32[8,4,4,512]{3,2,1,0:T(4,128)S(1)}, u32[]{:S(2)}, u32[]{:S(2)}) collective-permute-start(f32[8,4,4,512]{3,2,1,0:T(4,128)S(1)} %slice_select_fusion.5), channel_id=1, source_target_pairs={{0,4},{1,5},{2,6},{3,7},{4,0},{5,1},{6,2},{7,3},{8,12},{9,13},{10,... | collective-permute-start | bytes 786440 | tf_op jit(solution)/shard_map/ppermute | solution.py:17
  435.8 11.5 %collective-permute-done.4 = f32[8,4,4,512]{3,2,1,0:T(4,128)S(1)} collective-permute-done((f32[8,4,4,512]{3,2,1,0:T(4,128)S(1)}, f32[8,4,4,512]{3,2,1,0:T(4,128)S(1)}, u32[]{:S(2)}, u32[]{:S(2)}) %collective-permute-start.4) | collective-permute-done | bytes 262176 | tf_op jit(solution)/shard_map/ppermute | solution.py:17
  447.8 9.1 %collective-permute-start.5 = (f32[8,4,2,512]{3,2,1,0:T(2,128)S(1)}, f32[8,4,2,512]{3,2,1,0:T(2,128)S(1)}, u32[]{:S(2)}, u32[]{:S(2)}) collective-permute-start(f32[8,4,2,512]{3,2,1,0:T(2,128)S(1)} %broadcast_select_fusion.4), channel_id=1, source_target_pairs={{0,8},{1,9},{2,10},{3,11},{4,12},{5,13},{6,14},{7,15},{8,0},{9,1},... | collective-permute-start | bytes 393224 | tf_op jit(solution)/shard_map/ppermute | solution.py:17
  456.9 10.1 %collective-permute-done.5 = f32[8,4,2,512]{3,2,1,0:T(2,128)S(1)} collective-permute-done((f32[8,4,2,512]{3,2,1,0:T(2,128)S(1)}, f32[8,4,2,512]{3,2,1,0:T(2,128)S(1)}, u32[]{:S(2)}, u32[]{:S(2)}) %collective-permute-start.5) | collective-permute-done | bytes 131104 | tf_op jit(solution)/shard_map/ppermute | solution.py:17
  467.4 13.3 %collective-permute-start.6 = (f32[8,4,1,512]{3,1,0,2:T(4,128)S(1)}, f32[8,4,1,512]{3,1,0,2:T(4,128)S(1)}, u32[]{:S(2)}, u32[]{:S(2)}) collective-permute-start(f32[8,4,1,512]{3,1,0,2:T(4,128)S(1)} %slice_select_fusion.7), channel_id=1, source_target_pairs={{0,16},{1,17},{2,18},{3,19},{4,20},{5,21},{6,22},{7,23},{8,24},{9,... | collective-permute-start | bytes 196616 | tf_op jit(solution)/shard_map/ppermute | solution.py:17
  480.7 2.9 collective-permute-done.6
  (385 shorter events, 129.0 us)
Async XLA Ops:
  0.0 3.2 copy-start.48
  9.7 3.3 copy-start
  11.8 3.7 copy-start.2
  11.8 3.7 copy-start.32
  18.3 12.2 %collective-permute-start.1 = (f32[4,8,2048]{2,1,0:T(8,128)}, f32[4,8,2048]{2,1,0:T(8,128)S(1)}, u32[]{:S(2)}, u32[]{:S(2)}) collective-permute-start(f32[4,8,2048]{2,1,0:T(8,128)} %get-tuple-element.634), channel_id=1, source_target_pairs={{0,32},{32,64},{64,96},{96,128},{128,160},{160,192},{192,224},{224... | collective-permute-start | bytes 786440 | tf_op jit(solution)/shard_map/while/body/eval_jaxpr/ppermute | solution.py:23
  31.6 11.4 %collective-permute-start.1 = (f32[4,8,2048]{2,1,0:T(8,128)}, f32[4,8,2048]{2,1,0:T(8,128)S(1)}, u32[]{:S(2)}, u32[]{:S(2)}) collective-permute-start(f32[4,8,2048]{2,1,0:T(8,128)} %get-tuple-element.634), channel_id=1, source_target_pairs={{0,32},{32,64},{64,96},{96,128},{128,160},{160,192},{192,224},{224... | collective-permute-start | bytes 786440 | tf_op jit(solution)/shard_map/while/body/eval_jaxpr/ppermute | solution.py:23
  44.0 10.6 %collective-permute-start.1 = (f32[4,8,2048]{2,1,0:T(8,128)}, f32[4,8,2048]{2,1,0:T(8,128)S(1)}, u32[]{:S(2)}, u32[]{:S(2)}) collective-permute-start(f32[4,8,2048]{2,1,0:T(8,128)} %get-tuple-element.634), channel_id=1, source_target_pairs={{0,32},{32,64},{64,96},{96,128},{128,160},{160,192},{192,224},{224... | collective-permute-start | bytes 786440 | tf_op jit(solution)/shard_map/while/body/eval_jaxpr/ppermute | solution.py:23
  55.7 10.6 %collective-permute-start.1 = (f32[4,8,2048]{2,1,0:T(8,128)}, f32[4,8,2048]{2,1,0:T(8,128)S(1)}, u32[]{:S(2)}, u32[]{:S(2)}) collective-permute-start(f32[4,8,2048]{2,1,0:T(8,128)} %get-tuple-element.634), channel_id=1, source_target_pairs={{0,32},{32,64},{64,96},{96,128},{128,160},{160,192},{192,224},{224... | collective-permute-start | bytes 786440 | tf_op jit(solution)/shard_map/while/body/eval_jaxpr/ppermute | solution.py:23
  67.3 10.6 %collective-permute-start.1 = (f32[4,8,2048]{2,1,0:T(8,128)}, f32[4,8,2048]{2,1,0:T(8,128)S(1)}, u32[]{:S(2)}, u32[]{:S(2)}) collective-permute-start(f32[4,8,2048]{2,1,0:T(8,128)} %get-tuple-element.634), channel_id=1, source_target_pairs={{0,32},{32,64},{64,96},{96,128},{128,160},{160,192},{192,224},{224... | collective-permute-start | bytes 786440 | tf_op jit(solution)/shard_map/while/body/eval_jaxpr/ppermute | solution.py:23
  78.9 10.6 %collective-permute-start.1 = (f32[4,8,2048]{2,1,0:T(8,128)}, f32[4,8,2048]{2,1,0:T(8,128)S(1)}, u32[]{:S(2)}, u32[]{:S(2)}) collective-permute-start(f32[4,8,2048]{2,1,0:T(8,128)} %get-tuple-element.634), channel_id=1, source_target_pairs={{0,32},{32,64},{64,96},{96,128},{128,160},{160,192},{192,224},{224... | collective-permute-start | bytes 786440 | tf_op jit(solution)/shard_map/while/body/eval_jaxpr/ppermute | solution.py:23
  90.6 10.6 %collective-permute-start.1 = (f32[4,8,2048]{2,1,0:T(8,128)}, f32[4,8,2048]{2,1,0:T(8,128)S(1)}, u32[]{:S(2)}, u32[]{:S(2)}) collective-permute-start(f32[4,8,2048]{2,1,0:T(8,128)} %get-tuple-element.634), channel_id=1, source_target_pairs={{0,32},{32,64},{64,96},{96,128},{128,160},{160,192},{192,224},{224... | collective-permute-start | bytes 786440 | tf_op jit(solution)/shard_map/while/body/eval_jaxpr/ppermute | solution.py:23
  102.2 11.5 %collective-permute-start.1 = (f32[4,8,2048]{2,1,0:T(8,128)}, f32[4,8,2048]{2,1,0:T(8,128)S(1)}, u32[]{:S(2)}, u32[]{:S(2)}) collective-permute-start(f32[4,8,2048]{2,1,0:T(8,128)} %get-tuple-element.634), channel_id=1, source_target_pairs={{0,32},{32,64},{64,96},{96,128},{128,160},{160,192},{192,224},{224... | collective-permute-start | bytes 786440 | tf_op jit(solution)/shard_map/while/body/eval_jaxpr/ppermute | solution.py:23
  114.8 12.6 %collective-permute-start.1 = (f32[4,8,2048]{2,1,0:T(8,128)}, f32[4,8,2048]{2,1,0:T(8,128)S(1)}, u32[]{:S(2)}, u32[]{:S(2)}) collective-permute-start(f32[4,8,2048]{2,1,0:T(8,128)} %get-tuple-element.634), channel_id=1, source_target_pairs={{0,32},{32,64},{64,96},{96,128},{128,160},{160,192},{192,224},{224... | collective-permute-start | bytes 786440 | tf_op jit(solution)/shard_map/while/body/eval_jaxpr/ppermute | solution.py:23
  128.5 13.0 %collective-permute-start.1 = (f32[4,8,2048]{2,1,0:T(8,128)}, f32[4,8,2048]{2,1,0:T(8,128)S(1)}, u32[]{:S(2)}, u32[]{:S(2)}) collective-permute-start(f32[4,8,2048]{2,1,0:T(8,128)} %get-tuple-element.634), channel_id=1, source_target_pairs={{0,32},{32,64},{64,96},{96,128},{128,160},{160,192},{192,224},{224... | collective-permute-start | bytes 786440 | tf_op jit(solution)/shard_map/while/body/eval_jaxpr/ppermute | solution.py:23
  142.5 12.1 %collective-permute-start.1 = (f32[4,8,2048]{2,1,0:T(8,128)}, f32[4,8,2048]{2,1,0:T(8,128)S(1)}, u32[]{:S(2)}, u32[]{:S(2)}) collective-permute-start(f32[4,8,2048]{2,1,0:T(8,128)} %get-tuple-element.634), channel_id=1, source_target_pairs={{0,32},{32,64},{64,96},{96,128},{128,160},{160,192},{192,224},{224... | collective-permute-start | bytes 786440 | tf_op jit(solution)/shard_map/while/body/eval_jaxpr/ppermute | solution.py:23
  155.7 11.3 %collective-permute-start.1 = (f32[4,8,2048]{2,1,0:T(8,128)}, f32[4,8,2048]{2,1,0:T(8,128)S(1)}, u32[]{:S(2)}, u32[]{:S(2)}) collective-permute-start(f32[4,8,2048]{2,1,0:T(8,128)} %get-tuple-element.634), channel_id=1, source_target_pairs={{0,32},{32,64},{64,96},{96,128},{128,160},{160,192},{192,224},{224... | collective-permute-start | bytes 786440 | tf_op jit(solution)/shard_map/while/body/eval_jaxpr/ppermute | solution.py:23
  168.1 10.6 %collective-permute-start.1 = (f32[4,8,2048]{2,1,0:T(8,128)}, f32[4,8,2048]{2,1,0:T(8,128)S(1)}, u32[]{:S(2)}, u32[]{:S(2)}) collective-permute-start(f32[4,8,2048]{2,1,0:T(8,128)} %get-tuple-element.634), channel_id=1, source_target_pairs={{0,32},{32,64},{64,96},{96,128},{128,160},{160,192},{192,224},{224... | collective-permute-start | bytes 786440 | tf_op jit(solution)/shard_map/while/body/eval_jaxpr/ppermute | solution.py:23
  179.7 10.6 %collective-permute-start.1 = (f32[4,8,2048]{2,1,0:T(8,128)}, f32[4,8,2048]{2,1,0:T(8,128)S(1)}, u32[]{:S(2)}, u32[]{:S(2)}) collective-permute-start(f32[4,8,2048]{2,1,0:T(8,128)} %get-tuple-element.634), channel_id=1, source_target_pairs={{0,32},{32,64},{64,96},{96,128},{128,160},{160,192},{192,224},{224... | collective-permute-start | bytes 786440 | tf_op jit(solution)/shard_map/while/body/eval_jaxpr/ppermute | solution.py:23
  191.3 10.6 %collective-permute-start.1 = (f32[4,8,2048]{2,1,0:T(8,128)}, f32[4,8,2048]{2,1,0:T(8,128)S(1)}, u32[]{:S(2)}, u32[]{:S(2)}) collective-permute-start(f32[4,8,2048]{2,1,0:T(8,128)} %get-tuple-element.634), channel_id=1, source_target_pairs={{0,32},{32,64},{64,96},{96,128},{128,160},{160,192},{192,224},{224... | collective-permute-start | bytes 786440 | tf_op jit(solution)/shard_map/while/body/eval_jaxpr/ppermute | solution.py:23
  203.9 173.6 %copy-start.39 = (f32[1,8,2048]{2,0,1:T(1,128)S(1)}, f32[1,8,2048]{2,0,1:T(1,128)}, u32[]{:S(2)}) copy-start(f32[1,8,2048]{2,0,1:T(1,128)} %get-tuple-element.381) | copy-start | bytes 196612
  203.9 11.0 %collective-permute-start = (f32[4,8,2048]{2,1,0:T(8,128)S(1)}, f32[4,8,2048]{2,1,0:T(8,128)S(1)}, u32[]{:S(2)}, u32[]{:S(2)}) collective-permute-start(f32[4,8,2048]{2,1,0:T(8,128)S(1)} %get-tuple-element.658), channel_id=1, source_target_pairs={{0,32},{32,64},{64,96},{96,128},{128,160},{160,192},{192,224},{224... | collective-permute-start | bytes 786440 | tf_op jit(solution)/shard_map/while/body/eval_jaxpr/ppermute | solution.py:23
  215.3 12.0 %collective-permute-start = (f32[4,8,2048]{2,1,0:T(8,128)S(1)}, f32[4,8,2048]{2,1,0:T(8,128)S(1)}, u32[]{:S(2)}, u32[]{:S(2)}) collective-permute-start(f32[4,8,2048]{2,1,0:T(8,128)S(1)} %get-tuple-element.658), channel_id=1, source_target_pairs={{0,32},{32,64},{64,96},{96,128},{128,160},{160,192},{192,224},{224... | collective-permute-start | bytes 786440 | tf_op jit(solution)/shard_map/while/body/eval_jaxpr/ppermute | solution.py:23
  227.7 13.1 %collective-permute-start = (f32[4,8,2048]{2,1,0:T(8,128)S(1)}, f32[4,8,2048]{2,1,0:T(8,128)S(1)}, u32[]{:S(2)}, u32[]{:S(2)}) collective-permute-start(f32[4,8,2048]{2,1,0:T(8,128)S(1)} %get-tuple-element.658), channel_id=1, source_target_pairs={{0,32},{32,64},{64,96},{96,128},{128,160},{160,192},{192,224},{224... | collective-permute-start | bytes 786440 | tf_op jit(solution)/shard_map/while/body/eval_jaxpr/ppermute | solution.py:23
  241.2 12.3 %collective-permute-start = (f32[4,8,2048]{2,1,0:T(8,128)S(1)}, f32[4,8,2048]{2,1,0:T(8,128)S(1)}, u32[]{:S(2)}, u32[]{:S(2)}) collective-permute-start(f32[4,8,2048]{2,1,0:T(8,128)S(1)} %get-tuple-element.658), channel_id=1, source_target_pairs={{0,32},{32,64},{64,96},{96,128},{128,160},{160,192},{192,224},{224... | collective-permute-start | bytes 786440 | tf_op jit(solution)/shard_map/while/body/eval_jaxpr/ppermute | solution.py:23
  253.9 11.5 %collective-permute-start = (f32[4,8,2048]{2,1,0:T(8,128)S(1)}, f32[4,8,2048]{2,1,0:T(8,128)S(1)}, u32[]{:S(2)}, u32[]{:S(2)}) collective-permute-start(f32[4,8,2048]{2,1,0:T(8,128)S(1)} %get-tuple-element.658), channel_id=1, source_target_pairs={{0,32},{32,64},{64,96},{96,128},{128,160},{160,192},{192,224},{224... | collective-permute-start | bytes 786440 | tf_op jit(solution)/shard_map/while/body/eval_jaxpr/ppermute | solution.py:23
  265.8 10.6 %collective-permute-start = (f32[4,8,2048]{2,1,0:T(8,128)S(1)}, f32[4,8,2048]{2,1,0:T(8,128)S(1)}, u32[]{:S(2)}, u32[]{:S(2)}) collective-permute-start(f32[4,8,2048]{2,1,0:T(8,128)S(1)} %get-tuple-element.658), channel_id=1, source_target_pairs={{0,32},{32,64},{64,96},{96,128},{128,160},{160,192},{192,224},{224... | collective-permute-start | bytes 786440 | tf_op jit(solution)/shard_map/while/body/eval_jaxpr/ppermute | solution.py:23
  276.8 10.4 %collective-permute-start = (f32[4,8,2048]{2,1,0:T(8,128)S(1)}, f32[4,8,2048]{2,1,0:T(8,128)S(1)}, u32[]{:S(2)}, u32[]{:S(2)}) collective-permute-start(f32[4,8,2048]{2,1,0:T(8,128)S(1)} %get-tuple-element.658), channel_id=1, source_target_pairs={{0,32},{32,64},{64,96},{96,128},{128,160},{160,192},{192,224},{224... | collective-permute-start | bytes 786440 | tf_op jit(solution)/shard_map/while/body/eval_jaxpr/ppermute | solution.py:23
  287.6 10.4 %collective-permute-start = (f32[4,8,2048]{2,1,0:T(8,128)S(1)}, f32[4,8,2048]{2,1,0:T(8,128)S(1)}, u32[]{:S(2)}, u32[]{:S(2)}) collective-permute-start(f32[4,8,2048]{2,1,0:T(8,128)S(1)} %get-tuple-element.658), channel_id=1, source_target_pairs={{0,32},{32,64},{64,96},{96,128},{128,160},{160,192},{192,224},{224... | collective-permute-start | bytes 786440 | tf_op jit(solution)/shard_map/while/body/eval_jaxpr/ppermute | solution.py:23
  298.3 10.4 %collective-permute-start = (f32[4,8,2048]{2,1,0:T(8,128)S(1)}, f32[4,8,2048]{2,1,0:T(8,128)S(1)}, u32[]{:S(2)}, u32[]{:S(2)}) collective-permute-start(f32[4,8,2048]{2,1,0:T(8,128)S(1)} %get-tuple-element.658), channel_id=1, source_target_pairs={{0,32},{32,64},{64,96},{96,128},{128,160},{160,192},{192,224},{224... | collective-permute-start | bytes 786440 | tf_op jit(solution)/shard_map/while/body/eval_jaxpr/ppermute | solution.py:23
  309.1 10.4 %collective-permute-start = (f32[4,8,2048]{2,1,0:T(8,128)S(1)}, f32[4,8,2048]{2,1,0:T(8,128)S(1)}, u32[]{:S(2)}, u32[]{:S(2)}) collective-permute-start(f32[4,8,2048]{2,1,0:T(8,128)S(1)} %get-tuple-element.658), channel_id=1, source_target_pairs={{0,32},{32,64},{64,96},{96,128},{128,160},{160,192},{192,224},{224... | collective-permute-start | bytes 786440 | tf_op jit(solution)/shard_map/while/body/eval_jaxpr/ppermute | solution.py:23
  319.9 11.6 %collective-permute-start = (f32[4,8,2048]{2,1,0:T(8,128)S(1)}, f32[4,8,2048]{2,1,0:T(8,128)S(1)}, u32[]{:S(2)}, u32[]{:S(2)}) collective-permute-start(f32[4,8,2048]{2,1,0:T(8,128)S(1)} %get-tuple-element.658), channel_id=1, source_target_pairs={{0,32},{32,64},{64,96},{96,128},{128,160},{160,192},{192,224},{224... | collective-permute-start | bytes 786440 | tf_op jit(solution)/shard_map/while/body/eval_jaxpr/ppermute | solution.py:23
  331.9 12.7 %collective-permute-start = (f32[4,8,2048]{2,1,0:T(8,128)S(1)}, f32[4,8,2048]{2,1,0:T(8,128)S(1)}, u32[]{:S(2)}, u32[]{:S(2)}) collective-permute-start(f32[4,8,2048]{2,1,0:T(8,128)S(1)} %get-tuple-element.658), channel_id=1, source_target_pairs={{0,32},{32,64},{64,96},{96,128},{128,160},{160,192},{192,224},{224... | collective-permute-start | bytes 786440 | tf_op jit(solution)/shard_map/while/body/eval_jaxpr/ppermute | solution.py:23
  345.0 10.4 %collective-permute-start = (f32[4,8,2048]{2,1,0:T(8,128)S(1)}, f32[4,8,2048]{2,1,0:T(8,128)S(1)}, u32[]{:S(2)}, u32[]{:S(2)}) collective-permute-start(f32[4,8,2048]{2,1,0:T(8,128)S(1)} %get-tuple-element.658), channel_id=1, source_target_pairs={{0,32},{32,64},{64,96},{96,128},{128,160},{160,192},{192,224},{224... | collective-permute-start | bytes 786440 | tf_op jit(solution)/shard_map/while/body/eval_jaxpr/ppermute | solution.py:23
  355.8 10.4 %collective-permute-start = (f32[4,8,2048]{2,1,0:T(8,128)S(1)}, f32[4,8,2048]{2,1,0:T(8,128)S(1)}, u32[]{:S(2)}, u32[]{:S(2)}) collective-permute-start(f32[4,8,2048]{2,1,0:T(8,128)S(1)} %get-tuple-element.658), channel_id=1, source_target_pairs={{0,32},{32,64},{64,96},{96,128},{128,160},{160,192},{192,224},{224... | collective-permute-start | bytes 786440 | tf_op jit(solution)/shard_map/while/body/eval_jaxpr/ppermute | solution.py:23
  366.6 10.4 %collective-permute-start = (f32[4,8,2048]{2,1,0:T(8,128)S(1)}, f32[4,8,2048]{2,1,0:T(8,128)S(1)}, u32[]{:S(2)}, u32[]{:S(2)}) collective-permute-start(f32[4,8,2048]{2,1,0:T(8,128)S(1)} %get-tuple-element.658), channel_id=1, source_target_pairs={{0,32},{32,64},{64,96},{96,128},{128,160},{160,192},{192,224},{224... | collective-permute-start | bytes 786440 | tf_op jit(solution)/shard_map/while/body/eval_jaxpr/ppermute | solution.py:23
  387.1 2.8 copy-start.23
  388.2 2.9 copy-start.49
  391.4 2.8 copy-start.13
  391.4 2.8 copy-start.14
  391.4 2.8 copy-start.29
  404.2 3.1 copy-start.52
  405.4 4.8 collective-permute-start.2
  412.0 5.5 %copy-start.51 = (s32[8]{0:T(128)S(1)}, s32[8]{0:T(128)}, u32[]{:S(2)}) copy-start(s32[8]{0:T(128)} %param.13) | copy-start | bytes 100
  412.0 17.7 %copy-start.50 = (pred[8]{0:T(512)(128)(4,1)S(1)}, pred[8]{0:T(512)(128)(4,1)}, u32[]{:S(2)}) copy-start(pred[8]{0:T(512)(128)(4,1)} %get-tuple-element.515) | copy-start | bytes 28
  413.7 16.0 %collective-permute-start.3 = (f32[8,4,8,512]{3,2,1,0:T(8,128)S(1)}, f32[8,4,8,512]{3,2,1,0:T(8,128)S(1)}, u32[]{:S(2)}, u32[]{:S(2)}) collective-permute-start(f32[8,4,8,512]{3,2,1,0:T(8,128)S(1)} %slice_select_fusion.3), channel_id=1, source_target_pairs={{0,2},{1,3},{2,0},{3,1},{4,6},{5,7},{6,4},{7,5},{8,10},{9,11},{10,... | collective-permute-start | bytes 1572872 | tf_op jit(solution)/shard_map/ppermute | solution.py:17
  430.5 16.7 %collective-permute-start.4 = (f32[8,4,4,512]{3,2,1,0:T(4,128)S(1)}, f32[8,4,4,512]{3,2,1,0:T(4,128)S(1)}, u32[]{:S(2)}, u32[]{:S(2)}) collective-permute-start(f32[8,4,4,512]{3,2,1,0:T(4,128)S(1)} %slice_select_fusion.5), channel_id=1, source_target_pairs={{0,4},{1,5},{2,6},{3,7},{4,0},{5,1},{6,2},{7,3},{8,12},{9,13},{10,... | collective-permute-start | bytes 786440 | tf_op jit(solution)/shard_map/ppermute | solution.py:17
  447.8 19.2 %collective-permute-start.5 = (f32[8,4,2,512]{3,2,1,0:T(2,128)S(1)}, f32[8,4,2,512]{3,2,1,0:T(2,128)S(1)}, u32[]{:S(2)}, u32[]{:S(2)}) collective-permute-start(f32[8,4,2,512]{3,2,1,0:T(2,128)S(1)} %broadcast_select_fusion.4), channel_id=1, source_target_pairs={{0,8},{1,9},{2,10},{3,11},{4,12},{5,13},{6,14},{7,15},{8,0},{9,1},... | collective-permute-start | bytes 393224 | tf_op jit(solution)/shard_map/ppermute | solution.py:17
  467.4 16.3 %collective-permute-start.6 = (f32[8,4,1,512]{3,1,0,2:T(4,128)S(1)}, f32[8,4,1,512]{3,1,0,2:T(4,128)S(1)}, u32[]{:S(2)}, u32[]{:S(2)}) collective-permute-start(f32[8,4,1,512]{3,1,0,2:T(4,128)S(1)} %slice_select_fusion.7), channel_id=1, source_target_pairs={{0,16},{1,17},{2,18},{3,19},{4,20},{5,21},{6,22},{7,23},{8,24},{9,... | collective-permute-start | bytes 196616 | tf_op jit(solution)/shard_map/ppermute | solution.py:17
  (41 other events, 66.1 us)
where the time goes:
time: 486 us; the launch traced here: 484 us
  waiting for transfers between devices  305 us (63%)
  starting transfers between devices  92.3 us (19%)
  other arithmetic  61.4 us (13%)
  local copies, waits for them, and re-layouts  22.8 us (5%)
    ppermute x30, waiting for transfers between devices, shifted(): lax.ppermute(value, axis, [(source, source + steps) for source in range(l...  266 us
    ppermute x30, starting transfers between devices, shifted(): lax.ppermute(value, axis, [(source, source + steps) for source in range(l...  59 us
    ppermute x5, waiting for transfers between devices, partner(): return lax.ppermute(value, axis, pairs)  39.1 us
    ppermute x5, starting transfers between devices, partner(): return lax.ppermute(value, axis, pairs)  33.3 us
    mul x30, other arithmetic, hop_once(): slide_cells(entering_now, lateral, slices) * exit_part  15.1 us
    slice x59, local copies, waits for them, and re-layouts, move_cells(): return jnp.concatenate([filler, planes[..., :columns - amount]], axis=-1)  10.6 us
    eq x31, other arithmetic, slide_cells(): lateral == 1  10.5 us
  transfers between devices with their start and end apart: 35, of which 35 were waited for; matrix products, arithmetic and copies ran while one was open for 2% of the time, Pallas kernels for 0%

commit v1 on v0

v1 whole, which is shorter than its diff:
```python
import jax
import jax.numpy as jnp
from jax import lax
from jax.experimental import pallas as pl
from jax.experimental.pallas import tpu as pltpu
from jax.sharding import PartitionSpec as P

LIGHTS = 8
LIGHT_DEPTH = 1.5
VIEW_DEPTH = 2.0
LANES = 128
STEPS = (-1, 0, 1)
ROWS = 40


def slide(planes, amount):
    if amount == 0:
        return planes
    columns = planes.shape[-1]
    rolled = pltpu.roll(planes, amount % columns, axis=1)
    lane = lax.broadcasted_iota(jnp.int32, (planes.shape[0], LANES), 1)
    if amount > 0:
        edge = jnp.where(lane >= amount, rolled[:, :LANES], 0.0)
        return jnp.concatenate([edge, rolled[:, LANES:]], axis=1)
    edge = jnp.where(lane < LANES + amount, rolled[:, columns - LANES :], 0.0)
    return jnp.concatenate([rolled[:, : columns - LANES], edge], axis=1)


def exit_kernel(scale, density_ref, exit_ref):
    slices, cells, columns = density_ref.shape
    for index, step in enumerate(STEPS):
        total = jnp.zeros((cells, columns), jnp.float32)
        for k in range(slices):
            total = slide(total + density_ref[k] * scale, step)
        exit_ref[index * cells : (index + 1) * cells, :] = total


def row_kernel(slices, rows_ref, total_ref):
    count, planes, columns = rows_ref.shape
    cells = planes // len(STEPS)
    for index, step in enumerate(STEPS):
        part = slice(index * cells, (index + 1) * cells)
        total = rows_ref[0, part, :]
        for x in range(1, count):
            total = slide(total, slices * step) + rows_ref[x, part, :]
        total_ref[part, :] = total


def gather_sums(parts, low):
    for bit, mask in enumerate(low):
        merged = []
        for i in range(0, len(parts), 2):
            a, b = parts[i], parts[i + 1]
            merged.append(jnp.where(mask, a, b) + pltpu.roll(jnp.where(mask, b, a), 1 << bit, axis=0))
        parts = merged
    return parts[0]


def brick_kernel(
    light_scale, view_scale, flip_ref, density_ref, albedo_ref, rows_ref, totals_ref, keep_ref, send_ref, depth_ref, lit_ref
):
    slices, cells, columns = density_ref.shape
    across = rows_ref.shape[0]
    light = lax.axis_index("light")
    place_x, place_y = lax.rem(light, across), light // across
    core = lax.rem(lax.axis_index("view"), 2)
    for index, step in enumerate(STEPS):
        part = slice(index * cells, (index + 1) * cells)
        entering = jnp.zeros((cells, columns), jnp.float32)
        for y in range(totals_ref.shape[0] - 1):
            entering = jnp.where(y < place_y, slide(entering, slices * across * step) + totals_ref[y, part, :], entering)
        for x in range(across - 1):
            entering = jnp.where(x < place_x, slide(entering, slices * step) + rows_ref[x, part, :], entering)
        depth_ref[index] = entering

    row = lax.broadcasted_iota(jnp.int32, (cells, LANES), 0)
    low = [(row & (1 << bit)) == 0 for bit in range(3)]
    row_wide = lax.broadcasted_iota(jnp.int32, (cells, columns), 0)
    mine_even = core == 0

    def one_slice(k, carry):
        dense = density_ref[k]
        flipped = flip_ref[k] == 1
        depth_view = dense * view_scale
        running = depth_view
        for reach in (1, 2, 4):
            running = running + jnp.where(row_wide >= reach, pltpu.roll(running, reach, axis=0), 0.0)
        total = jnp.broadcast_to(running[cells - 1 :, :], (cells, columns))
        ahead = jnp.where(flipped, total - running, running - depth_view)
        weights = jnp.exp(ahead) * (1.0 - jnp.exp(depth_view))
        dense_light = dense * light_scale
        for index, step in enumerate(STEPS):
            depth = depth_ref[index]
            lit_ref[index] = weights * jnp.exp(depth)
            depth_ref[index] = slide(depth + dense_light, step)
        for pair in range(columns // (8 * LANES)):
            chunks = []
            for chunk in (2 * pair, 2 * pair + 1):
                groups = [slice((4 * chunk + g) * LANES, (4 * chunk + g + 1) * LANES) for g in range(4)]
                reflect = [[albedo_ref[c, k, :, g].astype(jnp.float32) for g in groups] for c in range(3)]
                products = []
                for index in range(len(STEPS)):
                    lit = [lit_ref[index, :, g] for g in groups]
                    for c in range(3):
                        products += [reflect[c][g] * lit[g] for g in range(4)]
                products += [depth_view[:, g] for g in groups]
                tiles = [gather_sums(products[t : t + 8], low) for t in range(0, ROWS, 8)]
                tiles[-1] = jnp.where(low[2], tiles[-1], jnp.exp(jnp.where(low[2], 0.0, tiles[-1])))
                chunks.append(tiles)
            where = k * (columns // (8 * LANES)) + pair
            for t, (even, odd) in enumerate(zip(*chunks)):
                keep_ref[where, 8 * t : 8 * t + 8, :] = jnp.where(mine_even, even, odd)
                send_ref[where, 8 * t : 8 * t + 8, :] = jnp.where(mine_even, odd, even)
        return carry

    lax.fori_loop(0, slices, one_slice, 0)


def both_halves(tile, low):
    return jnp.where(low, pltpu.roll(tile, 4, axis=0), tile)


def over(front, back, low):
    through = both_halves(front[-1], low)
    out = [f + through * b for f, b in zip(front[:-1], back[:-1])]
    return out + [jnp.where(low, front[-1], 0.0) + through * back[-1]]


def tiles_of(ref, index):
    return [ref[index, 8 * t : 8 * t + 8, :] for t in range(ROWS // 8)]


def pair_kernel(per_slice, flip_ref, keep_ref, recv_ref, out_ref):
    low = lax.broadcasted_iota(jnp.int32, (8, LANES), 0) < 4
    core = lax.rem(lax.axis_index("view"), 2)

    def one_slice(k, carry):
        mine_front = core == flip_ref[k]
        for h in range(per_slice):
            where = k * per_slice + h
            keep, recv = tiles_of(keep_ref, where), tiles_of(recv_ref, where)
            front = [jnp.where(mine_front, a, b) for a, b in zip(keep, recv)]
            back = [jnp.where(mine_front, b, a) for a, b in zip(keep, recv)]
            for t, tile in enumerate(over(front, back, low)):
                out_ref[where, 8 * t : 8 * t + 8, :] = tile
        return carry

    lax.fori_loop(0, keep_ref.shape[0] // per_slice, one_slice, 0)


def final_kernel(per_slice, flip_ref, shift_ref, color_ref, pieces_ref, out_ref, sums_ref):
    low = lax.broadcasted_iota(jnp.int32, (8, LANES), 0) < 4
    count = pieces_ref.shape[0]
    flipped = flip_ref[lax.axis_index("view") // per_slice] == 1
    current = None
    for j in range(count):
        tiles = tiles_of(pieces_ref, jnp.where(flipped, count - 1 - j, j))
        current = tiles if current is None else over(current, tiles, low)
    for t, tile in enumerate(current):
        sums_ref[8 * t : 8 * t + 8, :] = tile
    for light in range(LIGHTS):
        base = (shift_ref[light] + 1) * 12
        for c in range(3):
            tint = color_ref[light, c]
            for g in range(4):
                out_ref[light, c : c + 1, g * LANES : (g + 1) * LANES] = sums_ref[pl.ds(base + 4 * c + g, 1), :] * tint
        for g in range(4):
            out_ref[light, 3:4, g * LANES : (g + 1) * LANES] = 1.0 - sums_ref[36 + g : 37 + g, :]


def vmem(count):
    return [pl.BlockSpec(memory_space=pltpu.VMEM)] * count


def smem(count):
    return [pl.BlockSpec(memory_space=pltpu.SMEM)] * count


def local(density, albedo, light_color, light_shift, view_flip):
    slices, cells, columns = density.shape
    light_count, view_count = lax.axis_size("light"), lax.axis_size("view")
    across = 4
    light_scale = -LIGHT_DEPTH / (slices * light_count)
    view_scale = -VIEW_DEPTH / (cells * view_count)
    planes = len(STEPS) * cells
    f32 = jnp.float32

    def call(kernel, name, out_shape, in_specs, scratch=()):
        many = isinstance(out_shape, (list, tuple))
        return pl.pallas_call(
            kernel,
            name=name,
            out_shape=out_shape,
            in_specs=in_specs,
            out_specs=vmem(len(out_shape)) if many else vmem(1)[0],
            scratch_shapes=scratch,
        )

    def shaped(*shape):
        return jax.ShapeDtypeStruct(shape, f32)

    rows_x = [[y * across + x for x in range(across)] for y in range(light_count // across)]
    rows_y = [[y * across + x for y in range(light_count // across)] for x in range(across)]
    leaving = call(lambda *refs: exit_kernel(light_scale, *refs), "exits", shaped(planes, columns), vmem(1))(density)
    in_row = lax.all_gather(leaving, "light", axis_index_groups=rows_x)
    total = call(lambda *refs: row_kernel(slices, *refs), "row_total", shaped(planes, columns), vmem(1))(in_row)
    totals = lax.all_gather(total, "light", axis_index_groups=rows_y)
    pieces = view_count // 2
    keep, send = call(
        lambda *refs: brick_kernel(light_scale, view_scale, *refs),
        "brick",
        [shaped(pieces, ROWS, LANES)] * 2,
        smem(1) + vmem(4),
        [pltpu.VMEM((len(STEPS), cells, columns), f32), pltpu.VMEM((len(STEPS), cells, columns), f32)],
    )(view_flip, density, albedo, in_row, totals)
    received = lax.ppermute(send, "view", [(v, v ^ 1) for v in range(view_count)])
    paired = call(
        lambda *refs: pair_kernel(pieces // slices, *refs), "pair", shaped(pieces, ROWS, LANES), smem(1) + vmem(2)
    )(view_flip, keep, received)
    groups = [[2 * z + c for z in range(pieces)] for c in range(2)]
    spread = lax.all_to_all(paired, "view", 0, 0, axis_index_groups=groups)
    return call(
        lambda *refs: final_kernel(view_count // slices, *refs),
        "final",
        shaped(LIGHTS, 4, slices * columns // view_count),
        smem(3) + vmem(1),
        [pltpu.VMEM((ROWS, LANES), f32)],
    )(view_flip, light_shift, light_color, spread)


def solution(mesh):
    return jax.shard_map(
        local,
        mesh=mesh,
        in_specs=(P("light", "view", None), P(None, "light", "view", None), P(), P(), P("light")),
        out_specs=P(None, None, ("light", "view")),
        check_vma=False,
    )
```

time: 486 us -> 86.2 us (0.18)
  the two profiles are of different devices: /device:TPU:16 before, /device:TPU:8 now
where the time goes in v1:
time: 86.2 us; the launch traced here: 85.7 us
  blocking collectives  33.4 us (39%)
  waiting for transfers between devices  22.5 us (26%)
  starting transfers between devices  14.6 us (17%)
  Pallas kernels  13 us (15%)
  local copies, waits for them, and re-layouts  2.15 us (2%)
    all_to_all x1, waiting for transfers between devices, local(): spread = lax.all_to_all(paired, 'view', 0, 0, axis_index_groups=groups)  20.7 us
    all_gather x1, blocking collectives, local(): totals = lax.all_gather(total, 'light', axis_index_groups=rows_y)  17.4 us
    all_gather x1, blocking collectives, local(): in_row = lax.all_gather(leaving, 'light', axis_index_groups=rows_x)  16 us
    all_to_all x1, starting transfers between devices, local(): spread = lax.all_to_all(paired, 'view', 0, 0, axis_index_groups=groups)  12.7 us
    pallas_call x1, Pallas kernels, local(): call(lambda *refs: brick_kernel(light_scale, view_scale, *refs), 'brick',...  4.85 us
    pallas_call x1, Pallas kernels, local(): call(lambda *refs: exit_kernel(light_scale, *refs), 'exits', shaped(plane...  2.36 us
    unnamed x7, local copies, waits for them, and re-layouts  2.15 us
    pallas_call x1, Pallas kernels, local(): call(lambda *refs: row_kernel(slices, *refs), 'row_total', shaped(planes,...  2.06 us
  transfers between devices with their start and end apart: 2, of which 2 were waited for; matrix products, arithmetic and copies ran while one was open for 1% of the time, Pallas kernels for 0%

profile of v1, /device:TPU:8, one launch (start us, length us, event | category | flops | bytes accessed | tf_op | source)
XLA Modules:
  0.0 85.7 jit_solution(16696591977078299180)
XLA Ops:
  0.0 2.4 %exits.1 = f32[24,2048]{1,0:T(8,128)} custom-call(f32[8,8,2048]{2,1,0:T(8,128)} %refs_1_.2), custom_call_target="tpu_custom_call" | custom-call | tf_op jit(solution)/shard_map/exits/pallas_call | solution.py:204
  2.4 16.0 %all-gather = f32[96,2048]{1,0:T(8,128)} all-gather(f32[24,2048]{1,0:T(8,128)} %exits.1), channel_id=2, replica_groups={{0,32,64,96},{128,160,192,224},{256,288,320,352},{384,416,448,480},{1,3..., dimensions={0}, use_global_device_ids=true | all-gather | bytes 983040 | tf_op jit(solution)/shard_map/all_gather | solution.py:205
  18.3 2.1 %row_total.1 = f32[24,2048]{1,0:T(8,128)} custom-call(f32[4,24,2048]{2,1,0:T(8,128)} %bitcast.2), custom_call_target="tpu_custom_call" | custom-call | tf_op jit(solution)/shard_map/row_total/pallas_call | solution.py:206
  20.4 17.4 %all-gather.1 = f32[96,2048]{1,0:T(8,128)} all-gather(f32[24,2048]{1,0:T(8,128)} %row_total.1), channel_id=3, replica_groups={{0,128,256,384},{32,160,288,416},{64,192,320,448},{96,224,352,480},{1,1..., dimensions={0}, use_global_device_ids=true | all-gather | bytes 983040 | tf_op jit(solution)/shard_map/all_gather | solution.py:207
  37.8 4.8 %brick.1 = (f32[16,40,128]{2,1,0:T(8,128)}, f32[16,40,128]{2,1,0:T(8,128)}) custom-call(s32[8]{0:T(128)} %refs_0_.7, f32[8,8,2048]{2,1,0:T(8,128)} %refs_1_.2, bf16[3,8,8,2048]{3,2,1,0:T(8,128)(2,1)} %refs_2_.2, f32[4,24,2048]{2,1,0:T(8,128)} %bitcast.3, f32[4,24,2048]{2,1,0:T(8,128)} %bitcast.4), custom_call_target="tpu_custom_call" | custom-call | tf_op jit(solution)/shard_map/brick/pallas_call | solution.py:209
  42.7 1.9 %collective-permute-start = (f32[16,40,128]{2,1,0:T(8,128)}, f32[16,40,128]{2,1,0:T(8,128)S(1)}, u32[]{:S(2)}, u32[]{:S(2)}) collective-permute-start(f32[16,40,128]{2,1,0:T(8,128)} %get-tuple-element.8), channel_id=1, source_target_pairs={{0,1},{1,0},{2,3},{3,2},{4,5},{5,4},{6,7},{7,6},{8,9},{9,8},{10,11... | collective-permute-start | bytes 983048 | tf_op jit(solution)/shard_map/ppermute | solution.py:216
  44.6 1.8 %collective-permute-done.refs_2_ = f32[16,40,128]{2,1,0:T(8,128)S(1)} collective-permute-done((f32[16,40,128]{2,1,0:T(8,128)}, f32[16,40,128]{2,1,0:T(8,128)S(1)}, u32[]{:S(2)}, u32[]{:S(2)}) %collective-permute-start) | collective-permute-done | bytes 327712 | tf_op jit(solution)/shard_map/ppermute | solution.py:216
  46.4 0.0 copy-start.1
  46.4 0.7 copy-done.1
  47.1 1.9 %pair.1 = f32[16,40,128]{2,1,0:T(8,128)} custom-call(s32[8]{0:T(128)} %refs_0_.7, f32[16,40,128]{2,1,0:T(8,128)} %get-tuple-element.7.refs_1_, f32[16,40,128]{2,1,0:T(8,128)} %copy-done.1), custom_call_target="tpu_custom_call" | custom-call | tf_op jit(solution)/shard_map/pair/pallas_call | solution.py:217
  49.1 0.0 copy-start.2
  49.1 12.7 %all-to-all-start = ((f32[16,40,128]{2,1,0:T(8,128)}), f32[16,40,128]{2,1,0:T(8,128)S(1)}, u32[]{:S(2)}, u32[]{:S(2)}) async-start(f32[16,40,128]{2,1,0:T(8,128)} %pair.1), calls=%async_computation | async-start | bytes 655360 | tf_op jit(solution)/shard_map/all_to_all | solution.py:221
  61.8 0.0 copy-done.2
  61.8 0.7 copy.6.refs_2_
  62.5 20.7 %all-to-all-done.refs_3_ = f32[16,40,128]{2,1,0:T(8,128)S(1)} async-done(((f32[16,40,128]{2,1,0:T(8,128)}), f32[16,40,128]{2,1,0:T(8,128)S(1)}, u32[]{:S(2)}, u32[]{:S(2)}) %all-to-all-start) | async-done | bytes 327712 | tf_op jit(solution)/shard_map/all_to_all | solution.py:221
  83.2 0.0 copy-start
  83.2 0.7 copy-done
  83.9 1.7 %final.1 = f32[8,4,512]{2,1,0:T(4,128)} custom-call(s32[8]{0:T(128)} %refs_0_.7, s32[8]{0:T(128)} %refs_1_.3, f32[8,3]{1,0:T(8,128)} %copy.6.refs_2_, f32[16,40,128]{2,1,0:T(8,128)} %copy-done), custom_call_target="tpu_custom_call" | custom-call | tf_op jit(solution)/shard_map/final/pallas_call | solution.py:222
Async XLA Ops:
  42.7 3.7 %collective-permute-start = (f32[16,40,128]{2,1,0:T(8,128)}, f32[16,40,128]{2,1,0:T(8,128)S(1)}, u32[]{:S(2)}, u32[]{:S(2)}) collective-permute-start(f32[16,40,128]{2,1,0:T(8,128)} %get-tuple-element.8), channel_id=1, source_target_pairs={{0,1},{1,0},{2,3},{3,2},{4,5},{5,4},{6,7},{7,6},{8,9},{9,8},{10,11... | collective-permute-start | bytes 983048 | tf_op jit(solution)/shard_map/ppermute | solution.py:216
  46.4 0.7 copy-start.1
  49.1 12.7 %copy-start.2 = (f32[8,3]{0,1:T(4,128)S(1)}, f32[8,3]{0,1:T(4,128)}, u32[]{:S(2)}) copy-start(f32[8,3]{0,1:T(4,128)} %param.7) | copy-start | bytes 292
  49.1 34.1 %all-to-all-start = ((f32[16,40,128]{2,1,0:T(8,128)}), f32[16,40,128]{2,1,0:T(8,128)S(1)}, u32[]{:S(2)}, u32[]{:S(2)}) async-start(f32[16,40,128]{2,1,0:T(8,128)} %pair.1), calls=%async_computation | async-start | bytes 655360 | tf_op jit(solution)/shard_map/all_to_all | solution.py:221
  83.2 0.7 copy-start

commit v2 on v1

--- a/solution.py
+++ b/solution.py
@@ -26,24 +26,45 @@
     return jnp.concatenate([rolled[:, : columns - LANES], edge], axis=1)
 
 
+def turn(groups, amount, forward):
+    lane = lax.broadcasted_iota(jnp.int32, groups[0].shape, 1)
+    if forward:
+        spun = [pltpu.roll(g, lax.rem(amount, LANES), axis=1) for g in groups]
+        return [jnp.where(lane >= amount, g, spun[i - 1]) for i, g in enumerate(spun)]
+    spun = [pltpu.roll(g, lax.rem(LANES - amount, LANES), axis=1) for g in groups]
+    return [jnp.where(lane < LANES - amount, g, spun[(i + 1) % len(spun)]) for i, g in enumerate(spun)]
+
+
 def exit_kernel(scale, density_ref, exit_ref):
     slices, cells, columns = density_ref.shape
+    count = exit_ref.shape[0]
+    amount = slices * (count - 1 - lax.axis_index("light"))
     for index, step in enumerate(STEPS):
         total = jnp.zeros((cells, columns), jnp.float32)
         for k in range(slices):
             total = slide(total + density_ref[k] * scale, step)
-        exit_ref[index * cells : (index + 1) * cells, :] = total
-
-
-def row_kernel(slices, rows_ref, total_ref):
-    count, planes, columns = rows_ref.shape
+        groups = [total[:, g * LANES : (g + 1) * LANES] for g in range(count)]
+        if step:
+            groups = turn(groups, amount, step > 0)
+        for g, values in enumerate(groups):
+            exit_ref[g, index * cells : (index + 1) * cells, :] = values
+
+
+def prefix_kernel(slices, leaving_ref, entering_ref):
+    count, planes, _ = leaving_ref.shape
     cells = planes // len(STEPS)
+    columns = count * LANES
+    place = lax.axis_index("light") * LANES + lax.broadcasted_iota(jnp.int32, (cells, LANES), 1)
     for index, step in enumerate(STEPS):
         part = slice(index * cells, (index + 1) * cells)
-        total = rows_ref[0, part, :]
-        for x in range(1, count):
-            total = slide(total, slices * step) + rows_ref[x, part, :]
-        total_ref[part, :] = total
+        total = jnp.zeros((cells, LANES), jnp.float32)
+        for j in range(count):
+            entering_ref[j, part, :] = total
+            if step and j:
+                column = (place - step * slices * (count - 1 - j) + columns) & (columns - 1)
+                fresh = column < slices if step > 0 else column >= columns - slices
+                total = jnp.where(fresh, 0.0, total)
+            total = total + leaving_ref[j, part, :]
 
 
 def gather_sums(parts, low):
@@ -56,22 +77,17 @@
     return parts[0]
 
 
-def brick_kernel(
-    light_scale, view_scale, flip_ref, density_ref, albedo_ref, rows_ref, totals_ref, keep_ref, send_ref, depth_ref, lit_ref
-):
+def brick_kernel(light_scale, view_scale, flip_ref, density_ref, albedo_ref, entering_ref, keep_ref, send_ref, depth_ref, lit_ref):
     slices, cells, columns = density_ref.shape
-    across = rows_ref.shape[0]
+    count = entering_ref.shape[0]
+    core = lax.rem(lax.axis_index("view"), 2)
     light = lax.axis_index("light")
-    place_x, place_y = lax.rem(light, across), light // across
-    core = lax.rem(lax.axis_index("view"), 2)
     for index, step in enumerate(STEPS):
-        part = slice(index * cells, (index + 1) * cells)
-        entering = jnp.zeros((cells, columns), jnp.float32)
-        for y in range(totals_ref.shape[0] - 1):
-            entering = jnp.where(y < place_y, slide(entering, slices * across * step) + totals_ref[y, part, :], entering)
-        for x in range(across - 1):
-            entering = jnp.where(x < place_x, slide(entering, slices * step) + rows_ref[x, part, :], entering)
-        depth_ref[index] = entering
+        groups = [entering_ref[g, index * cells : (index + 1) * cells, :] for g in range(count)]
+        if step:
+            groups = turn(groups, slices * (count - light), step < 0)
+        for g, values in enumerate(groups):
+            depth_ref[index, :, g * LANES : (g + 1) * LANES] = values
 
     row = lax.broadcasted_iota(jnp.int32, (cells, LANES), 0)
     low = [(row & (1 << bit)) == 0 for bit in range(3)]
@@ -107,10 +123,9 @@
                 tiles = [gather_sums(products[t : t + 8], low) for t in range(0, ROWS, 8)]
                 tiles[-1] = jnp.where(low[2], tiles[-1], jnp.exp(jnp.where(low[2], 0.0, tiles[-1])))
                 chunks.append(tiles)
-            where = k * (columns // (8 * LANES)) + pair
             for t, (even, odd) in enumerate(zip(*chunks)):
-                keep_ref[where, 8 * t : 8 * t + 8, :] = jnp.where(mine_even, even, odd)
-                send_ref[where, 8 * t : 8 * t + 8, :] = jnp.where(mine_even, odd, even)
+                keep_ref[pair, k, 8 * t : 8 * t + 8, :] = jnp.where(mine_even, even, odd)
+                send_ref[pair, k, 8 * t : 8 * t + 8, :] = jnp.where(mine_even, odd, even)
         return carry
 
     lax.fori_loop(0, slices, one_slice, 0)
@@ -126,26 +141,33 @@
     return out + [jnp.where(low, front[-1], 0.0) + through * back[-1]]
 
 
-def tiles_of(ref, index):
-    return [ref[index, 8 * t : 8 * t + 8, :] for t in range(ROWS // 8)]
-
-
-def pair_kernel(per_slice, flip_ref, keep_ref, recv_ref, out_ref):
+def tiles_of(ref, *index):
+    return [ref[(*index, slice(8 * t, 8 * t + 8))] for t in range(ROWS // 8)]
+
+
+def merge(ref, other_ref, index, other_index, mine_front, low):
+    mine, other = tiles_of(ref, *index), tiles_of(other_ref, *other_index)
+    front = [jnp.where(mine_front, a, b) for a, b in zip(mine, other)]
+    back = [jnp.where(mine_front, b, a) for a, b in zip(mine, other)]
+    return over(front, back, low)
+
+
+def core_kernel(flip_ref, keep_ref, both_ref, out_ref):
     low = lax.broadcasted_iota(jnp.int32, (8, LANES), 0) < 4
     core = lax.rem(lax.axis_index("view"), 2)
-
-    def one_slice(k, carry):
+    halves, slices = keep_ref.shape[:2]
+    for k in range(slices):
         mine_front = core == flip_ref[k]
-        for h in range(per_slice):
-            where = k * per_slice + h
-            keep, recv = tiles_of(keep_ref, where), tiles_of(recv_ref, where)
-            front = [jnp.where(mine_front, a, b) for a, b in zip(keep, recv)]
-            back = [jnp.where(mine_front, b, a) for a, b in zip(keep, recv)]
-            for t, tile in enumerate(over(front, back, low)):
-                out_ref[where, 8 * t : 8 * t + 8, :] = tile
-        return carry
-
-    lax.fori_loop(0, keep_ref.shape[0] // per_slice, one_slice, 0)
+        for h in range(halves):
+            for t, tile in enumerate(merge(keep_ref, both_ref, (h, k), (1 - core, h, k), mine_front, low)):
+                out_ref[h, k, 8 * t : 8 * t + 8, :] = tile
+
+
+def chip_kernel(flip_ref, both_ref, out_ref):
+    low = lax.broadcasted_iota(jnp.int32, (8, LANES), 0) < 4
+    for k in range(both_ref.shape[1]):
+        for t, tile in enumerate(merge(both_ref, both_ref, (0, k), (1, k), flip_ref[k] == 0, low)):
+            out_ref[k, 8 * t : 8 * t + 8, :] = tile
 
 
 def final_kernel(per_slice, flip_ref, shift_ref, color_ref, pieces_ref, out_ref, sums_ref):
@@ -179,7 +201,6 @@
 def local(density, albedo, light_color, light_shift, view_flip):
     slices, cells, columns = density.shape
     light_count, view_count = lax.axis_size("light"), lax.axis_size("view")
-    across = 4
     light_scale = -LIGHT_DEPTH / (slices * light_count)
     view_scale = -VIEW_DEPTH / (cells * view_count)
     planes = len(STEPS) * cells
@@ -194,38 +215,39 @@
             in_specs=in_specs,
             out_specs=vmem(len(out_shape)) if many else vmem(1)[0],
             scratch_shapes=scratch,
+            compiler_params=pltpu.CompilerParams(vmem_limit_bytes=16 * 2**20),
         )
 
     def shaped(*shape):
         return jax.ShapeDtypeStruct(shape, f32)
 
-    rows_x = [[y * across + x for x in range(across)] for y in range(light_count // across)]
-    rows_y = [[y * across + x for y in range(light_count // across)] for x in range(across)]
-    leaving = call(lambda *refs: exit_kernel(light_scale, *refs), "exits", shaped(planes, columns), vmem(1))(density)
-    in_row = lax.all_gather(leaving, "light", axis_index_groups=rows_x)
-    total = call(lambda *refs: row_kernel(slices, *refs), "row_total", shaped(planes, columns), vmem(1))(in_row)
-    totals = lax.all_gather(total, "light", axis_index_groups=rows_y)
-    pieces = view_count // 2
+    lines = shaped(light_count, planes, columns // light_count)
+    leaving = call(lambda *refs: exit_kernel(light_scale, *refs), "exits", lines, vmem(1))(density)
+    leaving = lax.all_to_all(leaving, "light", 0, 0)
+    entering = call(lambda *refs: prefix_kernel(slices, *refs), "prefix", lines, vmem(1))(leaving)
+    entering = lax.all_to_all(entering, "light", 0, 0)
     keep, send = call(
         lambda *refs: brick_kernel(light_scale, view_scale, *refs),
         "brick",
-        [shaped(pieces, ROWS, LANES)] * 2,
-        smem(1) + vmem(4),
+        [shaped(2, slices, ROWS, LANES)] * 2,
+        smem(1) + vmem(3),
         [pltpu.VMEM((len(STEPS), cells, columns), f32), pltpu.VMEM((len(STEPS), cells, columns), f32)],
-    )(view_flip, density, albedo, in_row, totals)
-    received = lax.ppermute(send, "view", [(v, v ^ 1) for v in range(view_count)])
-    paired = call(
-        lambda *refs: pair_kernel(pieces // slices, *refs), "pair", shaped(pieces, ROWS, LANES), smem(1) + vmem(2)
-    )(view_flip, keep, received)
-    groups = [[2 * z + c for z in range(pieces)] for c in range(2)]
-    spread = lax.all_to_all(paired, "view", 0, 0, axis_index_groups=groups)
+    )(view_flip, density, albedo, entering)
+    cores = [[2 * z, 2 * z + 1] for z in range(view_count // 2)]
+    both = lax.all_gather(send, "view", axis_index_groups=cores)
+    merged = call(core_kernel, "cores", shaped(2, slices, ROWS, LANES), smem(1) + vmem(2))(view_flip, keep, both)
+    chips = [[v, v + 2] for v in range(view_count) if v & 2 == 0]
+    both = lax.all_to_all(merged, "view", 0, 0, axis_index_groups=chips)
+    merged = call(chip_kernel, "chips", shaped(slices, ROWS, LANES), smem(1) + vmem(1))(view_flip, both)
+    rest = [[4 * k + r for k in range(slices)] for r in range(4)]
+    pieces = lax.all_to_all(merged, "view", 0, 0, axis_index_groups=rest)
     return call(
         lambda *refs: final_kernel(view_count // slices, *refs),
         "final",
         shaped(LIGHTS, 4, slices * columns // view_count),
         smem(3) + vmem(1),
         [pltpu.VMEM((ROWS, LANES), f32)],
-    )(view_flip, light_shift, light_color, spread)
+    )(view_flip, light_shift, light_color, pieces)
 
 
 def solution(mesh):

time: 86.2 us -> 76.2 us (0.88)
  the two profiles are of different devices: /device:TPU:8 before, /device:TPU:2 now
where the time goes in v2:
time: 76.2 us; the launch traced here: 75.9 us
  blocking collectives  37.9 us (50%)
  waiting for transfers between devices  16.3 us (21%)
  starting transfers between devices  14.1 us (19%)
  Pallas kernels  6.33 us (8%)
  local copies, waits for them, and re-layouts  1.15 us (2%)
    all_to_all x1, waiting for transfers between devices, local(): pieces = lax.all_to_all(merged, 'view', 0, 0, axis_index_groups=rest)  16.3 us
    all_to_all x1, blocking collectives, local(): leaving = lax.all_to_all(leaving, 'light', 0, 0)  15.5 us
    all_to_all x1, starting transfers between devices, local(): pieces = lax.all_to_all(merged, 'view', 0, 0, axis_index_groups=rest)  14.1 us
    all_to_all x1, blocking collectives, local(): entering = lax.all_to_all(entering, 'light', 0, 0)  11.3 us
    all_to_all x1, blocking collectives, local(): both = lax.all_to_all(merged, 'view', 0, 0, axis_index_groups=chips)  8.84 us
    pallas_call x1, Pallas kernels, local(): call(lambda *refs: brick_kernel(light_scale, view_scale, *refs), 'brick',...  2.41 us
    all_gather x1, blocking collectives, local(): both = lax.all_gather(send, 'view', axis_index_groups=cores)  2.28 us
  transfers between devices with their start and end apart: 1, of which 1 were waited for; matrix products, arithmetic and copies ran while one was open for 0% of the time, Pallas kernels for 0%

profile of v2, /device:TPU:2, one launch (start us, length us, event | category | flops | bytes accessed | tf_op | source)
XLA Modules:
  0.0 75.9 jit_solution(6085978573266209316)
XLA Ops:
  0.0 0.0 copy-start
  0.0 1.0 %copy-done = f32[8,8,2048]{2,1,0:T(8,128)S(1)} copy-done((f32[8,8,2048]{2,1,0:T(8,128)S(1)}, f32[8,8,2048]{2,1,0:T(8,128)}, u32[]{:S(2)}) %copy-start) | copy-done | bytes 524312
  1.0 0.0 copy-start.2
  1.0 0.7 exits.1
  1.8 0.0 copy-start.1
  1.8 15.5 %all_to_all.20.refs_0_ = f32[16,24,128]{2,1,0:T(8,128)S(1)} all-to-all(f32[16,24,128]{2,1,0:T(8,128)S(1)} %exits.1), channel_id=1, replica_groups=mesh['light'=16,'view'=32] {'light'}, dimensions={0} | all-to-all | bytes 393216 | tf_op jit(solution)/shard_map/all_to_all | solution.py:226
  17.3 0.0 copy-start.3
  17.3 11.3 %all_to_all.21.refs_3_ = f32[16,24,128]{2,1,0:T(8,128)S(1)} all-to-all(f32[16,24,128]{2,1,0:T(8,128)S(1)} %prefix.1), channel_id=1, replica_groups=mesh['light'=16,'view'=32] {'light'}, dimensions={0} | all-to-all | bytes 393216 | tf_op jit(solution)/shard_map/all_to_all | solution.py:228
  28.6 0.0 copy-done.2
  28.6 0.0 copy-done.1
  28.7 0.0 copy-done.3
  28.7 2.4 %brick.1 = (f32[2,8,40,128]{3,2,1,0:T(8,128)S(1)}, f32[2,8,40,128]{3,2,1,0:T(8,128)S(1)}) custom-call(s32[8]{0:T(128)S(1)} %copy-done.3, f32[8,8,2048]{2,1,0:T(8,128)S(1)} %copy-done.1, bf16[3,8,8,2048]{3,2,1,0:T(8,128)(2,1)S(1)} %copy-done.2, f32[16,24,128]{2,1,0:T(8,128)S(1)} %all_to_all.21.refs_3_), custom_call_target="tpu_custom_call" | custom-call | tf_op jit(solution)/shard_map/brick/pallas_call | solution.py:229
  31.1 2.3 %all-gather = f32[4,8,40,128]{3,2,1,0:T(8,128)S(1)} all-gather(f32[2,8,40,128]{3,2,1,0:T(8,128)S(1)} %get-tuple-element.8), channel_id=2, replica_groups={{0,1},{2,3},{4,5},{6,7},{8,9},{10,11},{12,13},{14,15},{16,17},{18,19},{..., dimensions={0}, use_global_device_ids=true | all-gather | bytes 983040 | tf_op jit(solution)/shard_map/all_gather | solution.py:237
  33.4 0.6 cores.1
  34.0 8.8 %all_to_all.22.both_ref = f32[2,8,40,128]{3,2,1,0:T(8,128)S(1)} all-to-all(f32[2,8,40,128]{3,2,1,0:T(8,128)S(1)} %cores.1), channel_id=1, replica_groups={{0,2},{1,3},{4,6},{5,7},{8,10},{9,11},{12,14},{13,15},{16,18},{17,19},{..., dimensions={0} | all-to-all | bytes 655360 | tf_op jit(solution)/shard_map/all_to_all | solution.py:240
  42.8 1.2 %chips.1 = f32[8,40,128]{2,1,0:T(8,128)} custom-call(s32[8]{0:T(128)S(1)} %copy-done.3, f32[2,8,40,128]{3,2,1,0:T(8,128)S(1)} %all_to_all.22.both_ref), custom_call_target="tpu_custom_call" | custom-call | tf_op jit(solution)/shard_map/chips/pallas_call | solution.py:241
  44.0 0.0 copy-start.5
  44.0 14.1 %all-to-all-start.3 = ((f32[8,40,128]{2,1,0:T(8,128)}), f32[8,40,128]{2,1,0:T(8,128)S(1)}, u32[]{:S(2)}, u32[]{:S(2)}) async-start(f32[8,40,128]{2,1,0:T(8,128)} %chips.1), calls=%async_computation.3 | async-start | bytes 327680 | tf_op jit(solution)/shard_map/all_to_all | solution.py:243
  58.1 0.0 copy-done.5
  58.2 0.0 copy-start.4
  58.2 0.1 copy.7.refs_2_
  58.2 16.3 %all-to-all-done.3.refs_3_ = f32[8,40,128]{2,1,0:T(8,128)S(1)} async-done(((f32[8,40,128]{2,1,0:T(8,128)}), f32[8,40,128]{2,1,0:T(8,128)S(1)}, u32[]{:S(2)}, u32[]{:S(2)}) %all-to-all-start.3) | async-done | bytes 163872 | tf_op jit(solution)/shard_map/all_to_all | solution.py:243
  74.5 0.0 copy-done.4
  74.5 1.3 %final.1 = f32[8,4,512]{2,1,0:T(4,128)} custom-call(s32[8]{0:T(128)S(1)} %copy-done.3, s32[8]{0:T(128)S(1)} %copy-done.4, f32[8,3]{1,0:T(8,128)S(1)} %copy.7.refs_2_, f32[8,40,128]{2,1,0:T(8,128)S(1)} %all-to-all-done.3.refs_3_), custom_call_target="tpu_custom_call" | custom-call | tf_op jit(solution)/shard_map/final/pallas_call | solution.py:244
  (1 shorter events, 0.0 us)
Async XLA Ops:
  0.0 1.0 %copy-start = (f32[8,8,2048]{2,1,0:T(8,128)S(1)}, f32[8,8,2048]{2,1,0:T(8,128)}, u32[]{:S(2)}) copy-start(f32[8,8,2048]{2,1,0:T(8,128)} %refs_1_.2) | copy-start | bytes 1572868
  1.0 27.6 %copy-start.2 = (bf16[3,8,8,2048]{3,2,1,0:T(8,128)(2,1)S(1)}, bf16[3,8,8,2048]{3,2,1,0:T(8,128)(2,1)}, u32[]{:S(2)}) copy-start(bf16[3,8,8,2048]{3,2,1,0:T(8,128)(2,1)} %refs_2_.2) | copy-start | bytes 2359300
  1.8 26.9 %copy-start.1 = (f32[8,8,2048]{2,1,0:T(8,128)S(1)}, f32[8,8,2048]{2,1,0:T(8,128)}, u32[]{:S(2)}) copy-start(f32[8,8,2048]{2,1,0:T(8,128)} %refs_1_.2) | copy-start | bytes 1572868
  17.3 11.3 %copy-start.3 = (s32[8]{0:T(128)S(1)}, s32[8]{0:T(128)}, u32[]{:S(2)}) copy-start(s32[8]{0:T(128)} %refs_0_.5) | copy-start | bytes 100
  44.0 14.1 %copy-start.5 = (f32[8,3]{0,1:T(4,128)S(1)}, f32[8,3]{0,1:T(4,128)}, u32[]{:S(2)}) copy-start(f32[8,3]{0,1:T(4,128)} %param.7) | copy-start | bytes 292
  44.0 30.5 %all-to-all-start.3 = ((f32[8,40,128]{2,1,0:T(8,128)}), f32[8,40,128]{2,1,0:T(8,128)S(1)}, u32[]{:S(2)}, u32[]{:S(2)}) async-start(f32[8,40,128]{2,1,0:T(8,128)} %chips.1), calls=%async_computation.3 | async-start | bytes 327680 | tf_op jit(solution)/shard_map/all_to_all | solution.py:243
  58.2 16.4 %copy-start.4 = (s32[8]{0:T(128)S(1)}, s32[8]{0:T(128)}, u32[]{:S(2)}) copy-start(s32[8]{0:T(128)} %refs_1_.3) | copy-start | bytes 100

commit v3 on v2

--- a/solution.py
+++ b/solution.py
@@ -35,14 +35,20 @@
     return [jnp.where(lane < LANES - amount, g, spun[(i + 1) % len(spun)]) for i, g in enumerate(spun)]
 
 
-def exit_kernel(scale, density_ref, exit_ref):
+def exit_kernel(scale, density_ref, exit_ref, dense_ref, total_ref, arrived):
     slices, cells, columns = density_ref.shape
     count = exit_ref.shape[0]
+    copies = [pltpu.make_async_copy(density_ref.at[k], dense_ref.at[k], arrived.at[k]) for k in range(slices)]
+    for copy in copies:
+        copy.start()
     amount = slices * (count - 1 - lax.axis_index("light"))
+    for k in range(slices):
+        copies[k].wait()
+        dense = dense_ref[k] * scale
+        for index, step in enumerate(STEPS):
+            total_ref[index] = slide(total_ref[index] + dense if k else dense, step)
     for index, step in enumerate(STEPS):
-        total = jnp.zeros((cells, columns), jnp.float32)
-        for k in range(slices):
-            total = slide(total + density_ref[k] * scale, step)
+        total = total_ref[index]
         groups = [total[:, g * LANES : (g + 1) * LANES] for g in range(count)]
         if step:
             groups = turn(groups, amount, step > 0)
@@ -77,7 +83,9 @@
     return parts[0]
 
 
-def brick_kernel(light_scale, view_scale, flip_ref, density_ref, albedo_ref, entering_ref, keep_ref, send_ref, depth_ref, lit_ref):
+def brick_kernel(
+    light_scale, view_scale, flip_ref, shift_ref, color_ref, density_ref, albedo_ref, entering_ref, keep_ref, send_ref, depth_ref, lit_ref
+):
     slices, cells, columns = density_ref.shape
     count = entering_ref.shape[0]
     core = lax.rem(lax.axis_index("view"), 2)
@@ -135,38 +143,47 @@
     return jnp.where(low, pltpu.roll(tile, 4, axis=0), tile)
 
 
-def over(front, back, low):
-    through = both_halves(front[-1], low)
-    out = [f + through * b for f, b in zip(front[:-1], back[:-1])]
-    return out + [jnp.where(low, front[-1], 0.0) + through * back[-1]]
-
-
 def tiles_of(ref, *index):
     return [ref[(*index, slice(8 * t, 8 * t + 8))] for t in range(ROWS // 8)]
 
 
-def merge(ref, other_ref, index, other_index, mine_front, low):
-    mine, other = tiles_of(ref, *index), tiles_of(other_ref, *other_index)
+def composite(pieces, low):
+    through = None
+    for tiles in pieces:
+        own = both_halves(tiles[-1], low)
+        tiles = tiles[:-1] + [jnp.where(low, tiles[-1], 0.0)]
+        if through is None:
+            sums, through = tiles, own
+        else:
+            sums = [total + through * tile for total, tile in zip(sums, tiles)]
+            through = through * own
+    return sums[:-1] + [jnp.where(low, sums[-1], through)]
+
+
+def merge(mine, other, mine_front, low):
     front = [jnp.where(mine_front, a, b) for a, b in zip(mine, other)]
     back = [jnp.where(mine_front, b, a) for a, b in zip(mine, other)]
-    return over(front, back, low)
-
-
-def core_kernel(flip_ref, keep_ref, both_ref, out_ref):
+    return composite([front, back], low)
+
+
+def core_kernel(flip_ref, keep_ref, both_ref, mine_ref, send_ref):
     low = lax.broadcasted_iota(jnp.int32, (8, LANES), 0) < 4
-    core = lax.rem(lax.axis_index("view"), 2)
-    halves, slices = keep_ref.shape[:2]
-    for k in range(slices):
+    view = lax.axis_index("view")
+    core, chip = view & 1, (view >> 1) & 1
+    for k in range(keep_ref.shape[1]):
         mine_front = core == flip_ref[k]
-        for h in range(halves):
-            for t, tile in enumerate(merge(keep_ref, both_ref, (h, k), (1 - core, h, k), mine_front, low)):
-                out_ref[h, k, 8 * t : 8 * t + 8, :] = tile
-
-
-def chip_kernel(flip_ref, both_ref, out_ref):
+        for half, out_ref in ((chip, mine_ref), (1 - chip, send_ref)):
+            merged = merge(tiles_of(keep_ref, half, k), tiles_of(both_ref, 1 - core, half, k), mine_front, low)
+            for t, tile in enumerate(merged):
+                out_ref[k, 8 * t : 8 * t + 8, :] = tile
+
+
+def chip_kernel(flip_ref, mine_ref, both_ref, out_ref):
     low = lax.broadcasted_iota(jnp.int32, (8, LANES), 0) < 4
-    for k in range(both_ref.shape[1]):
-        for t, tile in enumerate(merge(both_ref, both_ref, (0, k), (1, k), flip_ref[k] == 0, low)):
+    chip = (lax.axis_index("view") >> 1) & 1
+    for k in range(mine_ref.shape[0]):
+        merged = merge(tiles_of(mine_ref, k), tiles_of(both_ref, 1 - chip, k), chip == flip_ref[k], low)
+        for t, tile in enumerate(merged):
             out_ref[k, 8 * t : 8 * t + 8, :] = tile
 
 
@@ -174,16 +191,13 @@
     low = lax.broadcasted_iota(jnp.int32, (8, LANES), 0) < 4
     count = pieces_ref.shape[0]
     flipped = flip_ref[lax.axis_index("view") // per_slice] == 1
-    current = None
-    for j in range(count):
-        tiles = tiles_of(pieces_ref, jnp.where(flipped, count - 1 - j, j))
-        current = tiles if current is None else over(current, tiles, low)
-    for t, tile in enumerate(current):
+    order = [jnp.where(flipped, count - 1 - j, j) for j in range(count)]
+    for t, tile in enumerate(composite([tiles_of(pieces_ref, j) for j in order], low)):
         sums_ref[8 * t : 8 * t + 8, :] = tile
     for light in range(LIGHTS):
         base = (shift_ref[light] + 1) * 12
         for c in range(3):
-            tint = color_ref[light, c]
+            tint = color_ref[c, light]
             for g in range(4):
                 out_ref[light, c : c + 1, g * LANES : (g + 1) * LANES] = sums_ref[pl.ds(base + 4 * c + g, 1), :] * tint
         for g in range(4):
@@ -222,23 +236,35 @@
         return jax.ShapeDtypeStruct(shape, f32)
 
     lines = shaped(light_count, planes, columns // light_count)
-    leaving = call(lambda *refs: exit_kernel(light_scale, *refs), "exits", lines, vmem(1))(density)
+    leaving = call(
+        lambda *refs: exit_kernel(light_scale, *refs),
+        "exits",
+        lines,
+        [pl.BlockSpec(memory_space=pltpu.HBM)],
+        [
+            pltpu.VMEM(density.shape, f32),
+            pltpu.VMEM((len(STEPS), cells, columns), f32),
+            pltpu.SemaphoreType.DMA((slices,)),
+        ],
+    )(pltpu.with_memory_space_constraint(density, pltpu.HBM))
     leaving = lax.all_to_all(leaving, "light", 0, 0)
     entering = call(lambda *refs: prefix_kernel(slices, *refs), "prefix", lines, vmem(1))(leaving)
     entering = lax.all_to_all(entering, "light", 0, 0)
+    color = light_color.T
     keep, send = call(
         lambda *refs: brick_kernel(light_scale, view_scale, *refs),
         "brick",
         [shaped(2, slices, ROWS, LANES)] * 2,
-        smem(1) + vmem(3),
+        smem(3) + vmem(3),
         [pltpu.VMEM((len(STEPS), cells, columns), f32), pltpu.VMEM((len(STEPS), cells, columns), f32)],
-    )(view_flip, density, albedo, entering)
+    )(view_flip, light_shift, color, density, albedo, entering)
     cores = [[2 * z, 2 * z + 1] for z in range(view_count // 2)]
     both = lax.all_gather(send, "view", axis_index_groups=cores)
-    merged = call(core_kernel, "cores", shaped(2, slices, ROWS, LANES), smem(1) + vmem(2))(view_flip, keep, both)
+    half = shaped(slices, ROWS, LANES)
+    mine, send = call(core_kernel, "cores", [half] * 2, smem(1) + vmem(2))(view_flip, keep, both)
     chips = [[v, v + 2] for v in range(view_count) if v & 2 == 0]
-    both = lax.all_to_all(merged, "view", 0, 0, axis_index_groups=chips)
-    merged = call(chip_kernel, "chips", shaped(slices, ROWS, LANES), smem(1) + vmem(1))(view_flip, both)
+    both = lax.all_gather(send, "view", axis_index_groups=chips)
+    merged = call(chip_kernel, "chips", half, smem(1) + vmem(2))(view_flip, mine, both)
     rest = [[4 * k + r for k in range(slices)] for r in range(4)]
     pieces = lax.all_to_all(merged, "view", 0, 0, axis_index_groups=rest)
     return call(
@@ -247,7 +273,7 @@
         shaped(LIGHTS, 4, slices * columns // view_count),
         smem(3) + vmem(1),
         [pltpu.VMEM((ROWS, LANES), f32)],
-    )(view_flip, light_shift, light_color, pieces)
+    )(view_flip, light_shift, color, pieces)
 
 
 def solution(mesh):

time: 76.2 us -> 74.4 us (0.976)
  blocking collectives: 37.9 us -> 66.5 us
  waiting for transfers between devices: 16.3 us -> 0 us
  starting transfers between devices: 14.1 us -> 0 us
    all_to_all x1, blocking collectives: 8.84 us -> 30.5 us  [local(): pieces = lax.all_to_all(merged, 'view', 0, 0, axis_index_groups=rest)]
    all_to_all x1 -> x0, waiting for transfers between devices: 16.3 us -> none  [local(): pieces = lax.all_to_all(merged, 'view', 0, 0, axis_index_groups=rest)]
    all_to_all x1 -> x0, starting transfers between devices: 14.1 us -> none  [local(): pieces = lax.all_to_all(merged, 'view', 0, 0, axis_index_groups=rest)]
    all_gather x0 -> x1, blocking collectives: none -> 6.91 us  [local(): both = lax.all_gather(send, 'view', axis_index_groups=chips)]
  transfers between devices with their start and end apart: 1 -> 0, of which waited for: 1 -> 0; matrix products, arithmetic and copies ran while one was open for 0% -> 0% of each run, Pallas kernels for 0% -> 0%
where the time goes in v3:
time: 74.4 us; the launch traced here: 74.1 us
  blocking collectives  66.5 us (89%)
  Pallas kernels  6.85 us (9%)
    all_to_all x1, blocking collectives, local(): pieces = lax.all_to_all(merged, 'view', 0, 0, axis_index_groups=rest)  30.5 us
    all_to_all x1, blocking collectives, local(): leaving = lax.all_to_all(leaving, 'light', 0, 0)  15.5 us
    all_to_all x1, blocking collectives, local(): entering = lax.all_to_all(entering, 'light', 0, 0)  11.3 us
    all_gather x1, blocking collectives, local(): both = lax.all_gather(send, 'view', axis_index_groups=chips)  6.91 us
    pallas_call x1, Pallas kernels, local(): call(lambda *refs: brick_kernel(light_scale, view_scale, *refs), 'brick',...  2.44 us
    all_gather x1, blocking collectives, local(): both = lax.all_gather(send, 'view', axis_index_groups=cores)  2.28 us
    pallas_call x1, Pallas kernels, local(): call(lambda *refs: exit_kernel(light_scale, *refs), 'exits', lines, [pl.B...  1.88 us

profile of v3, /device:TPU:2, one launch (start us, length us, event | category | flops | bytes accessed | tf_op | source)
XLA Modules:
  0.0 74.1 jit_solution(14761381631393656334)
XLA Ops:
  0.0 0.0 copy-start.1
  0.0 1.9 %exits.1 = f32[16,24,128]{2,1,0:T(8,128)S(1)} custom-call(f32[8,8,2048]{2,1,0:T(8,128)} %refs_3_.1), custom_call_target="tpu_custom_call" | custom-call | tf_op jit(solution)/shard_map/exits/pallas_call | solution.py:239
  1.9 0.0 copy-start
  1.9 15.5 %all_to_all.15.refs_0_ = f32[16,24,128]{2,1,0:T(8,128)S(1)} all-to-all(f32[16,24,128]{2,1,0:T(8,128)S(1)} %exits.1), channel_id=1, replica_groups=mesh['light'=16,'view'=32] {'light'}, dimensions={0} | all-to-all | bytes 393216 | tf_op jit(solution)/shard_map/all_to_all | solution.py:250
  17.4 0.0 copy-start.3
  17.4 11.3 %all_to_all.16.refs_5_ = f32[16,24,128]{2,1,0:T(8,128)S(1)} all-to-all(f32[16,24,128]{2,1,0:T(8,128)S(1)} %prefix.1), channel_id=1, replica_groups=mesh['light'=16,'view'=32] {'light'}, dimensions={0} | all-to-all | bytes 393216 | tf_op jit(solution)/shard_map/all_to_all | solution.py:252
  28.8 0.0 copy-start.2
  28.8 0.0 copy-start.4
  28.8 0.0 copy-done.1
  28.8 0.0 copy-done
  28.8 0.0 copy-done.3
  28.8 0.6 copy-done.2
  29.4 0.0 copy-done.4
  29.4 2.4 %brick.1 = (f32[2,8,40,128]{3,2,1,0:T(8,128)S(1)}, f32[2,8,40,128]{3,2,1,0:T(8,128)S(1)}) custom-call(s32[8]{0:T(128)S(1)} %copy-done.2, s32[8]{0:T(128)S(1)} %copy-done.4, f32[3,8]{1,0:T(4,128)S(1)} %bitcast.5, f32[8,8,2048]{2,1,0:T(8,128)S(1)} %copy-done, bf16[3,8,8,2048]{3,2,1,0:T(8,128)(2,1)S(1)} %copy-done.1, f32[16,24,128]{2,1,0:T(8,128)S(1)} %all_to_all.16.refs_5_), custom_call_target="tpu_custom_call" | custom-call | tf_op jit(solution)/shard_map/brick/pallas_call | solution.py:254
  31.9 2.3 %all-gather = f32[4,8,40,128]{3,2,1,0:T(8,128)S(1)} all-gather(f32[2,8,40,128]{3,2,1,0:T(8,128)S(1)} %get-tuple-element.10), channel_id=2, replica_groups={{0,1},{2,3},{4,5},{6,7},{8,9},{10,11},{12,13},{14,15},{16,17},{18,19},{..., dimensions={0}, use_global_device_ids=true | all-gather | bytes 983040 | tf_op jit(solution)/shard_map/all_gather | solution.py:262
  34.2 0.6 cores.1
  34.8 6.9 %all-gather.1 = f32[16,40,128]{2,1,0:T(8,128)S(1)} all-gather(f32[8,40,128]{2,1,0:T(8,128)S(1)} %get-tuple-element.12), channel_id=3, replica_groups={{0,2},{1,3},{4,6},{5,7},{8,10},{9,11},{12,14},{13,15},{16,18},{17,19},{..., dimensions={0}, use_global_device_ids=true | all-gather | bytes 491520 | tf_op jit(solution)/shard_map/all_gather | solution.py:266
  41.7 0.6 chips.1
  42.3 30.5 %all_to_all.17.refs_3_ = f32[8,40,128]{2,1,0:T(8,128)S(1)} all-to-all(f32[8,40,128]{2,1,0:T(8,128)S(1)} %chips.1), channel_id=1, replica_groups={{0,4,8,12,16,20,24,28},{1,5,9,13,17,21,25,29},{2,6,10,14,18,22,26,30},{..., dimensions={0} | all-to-all | bytes 327680 | tf_op jit(solution)/shard_map/all_to_all | solution.py:269
  72.8 1.3 %final.1 = f32[8,4,512]{2,1,0:T(4,128)} custom-call(s32[8]{0:T(128)S(1)} %copy-done.2, s32[8]{0:T(128)S(1)} %copy-done.4, f32[3,8]{1,0:T(4,128)S(1)} %bitcast.6, f32[8,40,128]{2,1,0:T(8,128)S(1)} %all_to_all.17.refs_3_), custom_call_target="tpu_custom_call" | custom-call | tf_op jit(solution)/shard_map/final/pallas_call | solution.py:270
  (1 shorter events, 0.0 us)
Async XLA Ops:
  0.0 28.8 %copy-start.1 = (bf16[3,8,8,2048]{3,2,1,0:T(8,128)(2,1)S(1)}, bf16[3,8,8,2048]{3,2,1,0:T(8,128)(2,1)}, u32[]{:S(2)}) copy-start(bf16[3,8,8,2048]{3,2,1,0:T(8,128)(2,1)} %refs_4_.1) | copy-start | bytes 2359300
  1.9 26.9 %copy-start = (f32[8,8,2048]{2,1,0:T(8,128)S(1)}, f32[8,8,2048]{2,1,0:T(8,128)}, u32[]{:S(2)}) copy-start(f32[8,8,2048]{2,1,0:T(8,128)} %refs_3_.1) | copy-start | bytes 1572868
  17.4 11.4 %copy-start.3 = (f32[8,3]{0,1:T(4,128)S(1)}, f32[8,3]{0,1:T(4,128)}, u32[]{:S(2)}) copy-start(f32[8,3]{0,1:T(4,128)} %param.7) | copy-start | bytes 292
  28.8 0.7 copy-start.2
  28.8 0.7 copy-start.4

commit v4 on v3

--- a/solution.py
+++ b/solution.py
@@ -11,6 +11,8 @@
 LANES = 128
 STEPS = (-1, 0, 1)
 ROWS = 40
+LIGHT_FIRST = 10
+VIEW_FIRST = 5
 
 
 def slide(planes, amount):
@@ -60,17 +62,19 @@
     count, planes, _ = leaving_ref.shape
     cells = planes // len(STEPS)
     columns = count * LANES
-    place = lax.axis_index("light") * LANES + lax.broadcasted_iota(jnp.int32, (cells, LANES), 1)
+    position = lax.rem(lax.axis_index("light") + count - LIGHT_FIRST, count)
+    place = position * LANES + lax.broadcasted_iota(jnp.int32, (cells, LANES), 1)
     for index, step in enumerate(STEPS):
         part = slice(index * cells, (index + 1) * cells)
         total = jnp.zeros((cells, LANES), jnp.float32)
         for j in range(count):
-            entering_ref[j, part, :] = total
+            member = (j - LIGHT_FIRST) % count
+            entering_ref[member, part, :] = total
             if step and j:
                 column = (place - step * slices * (count - 1 - j) + columns) & (columns - 1)
                 fresh = column < slices if step > 0 else column >= columns - slices
                 total = jnp.where(fresh, 0.0, total)
-            total = total + leaving_ref[j, part, :]
+            total = total + leaving_ref[member, part, :]
 
 
 def gather_sums(parts, low):
@@ -184,14 +188,14 @@
     for k in range(mine_ref.shape[0]):
         merged = merge(tiles_of(mine_ref, k), tiles_of(both_ref, 1 - chip, k), chip == flip_ref[k], low)
         for t, tile in enumerate(merged):
-            out_ref[k, 8 * t : 8 * t + 8, :] = tile
+            out_ref[(k - VIEW_FIRST) % mine_ref.shape[0], 8 * t : 8 * t + 8, :] = tile
 
 
 def final_kernel(per_slice, flip_ref, shift_ref, color_ref, pieces_ref, out_ref, sums_ref):
     low = lax.broadcasted_iota(jnp.int32, (8, LANES), 0) < 4
     count = pieces_ref.shape[0]
     flipped = flip_ref[lax.axis_index("view") // per_slice] == 1
-    order = [jnp.where(flipped, count - 1 - j, j) for j in range(count)]
+    order = [jnp.where(flipped, (count - 1 - j - VIEW_FIRST) % count, (j - VIEW_FIRST) % count) for j in range(count)]
     for t, tile in enumerate(composite([tiles_of(pieces_ref, j) for j in order], low)):
         sums_ref[8 * t : 8 * t + 8, :] = tile
     for light in range(LIGHTS):
@@ -247,9 +251,10 @@
             pltpu.SemaphoreType.DMA((slices,)),
         ],
     )(pltpu.with_memory_space_constraint(density, pltpu.HBM))
-    leaving = lax.all_to_all(leaving, "light", 0, 0)
+    along = [[(j + LIGHT_FIRST) % light_count for j in range(light_count)]]
+    leaving = lax.all_to_all(leaving, "light", 0, 0, axis_index_groups=along)
     entering = call(lambda *refs: prefix_kernel(slices, *refs), "prefix", lines, vmem(1))(leaving)
-    entering = lax.all_to_all(entering, "light", 0, 0)
+    entering = lax.all_to_all(entering, "light", 0, 0, axis_index_groups=along)
     color = light_color.T
     keep, send = call(
         lambda *refs: brick_kernel(light_scale, view_scale, *refs),
@@ -265,7 +270,7 @@
     chips = [[v, v + 2] for v in range(view_count) if v & 2 == 0]
     both = lax.all_gather(send, "view", axis_index_groups=chips)
     merged = call(chip_kernel, "chips", half, smem(1) + vmem(2))(view_flip, mine, both)
-    rest = [[4 * k + r for k in range(slices)] for r in range(4)]
+    rest = [[4 * ((k + VIEW_FIRST) % slices) + r for k in range(slices)] for r in range(4)]
     pieces = lax.all_to_all(merged, "view", 0, 0, axis_index_groups=rest)
     return call(
         lambda *refs: final_kernel(view_count // slices, *refs),

time: 74.4 us -> 65.6 us (0.88)
  the two profiles are of different devices: /device:TPU:2 before, /device:TPU:8 now
where the time goes in v4:
time: 65.6 us; the launch traced here: 65.3 us
  blocking collectives  57.7 us (88%)
  Pallas kernels  6.86 us (10%)
  local copies, waits for them, and re-layouts  0.67 us (1%)
    all_to_all x1, blocking collectives, local(): pieces = lax.all_to_all(merged, 'view', 0, 0, axis_index_groups=rest)  21.6 us
    all_to_all x1, blocking collectives, local(): leaving = lax.all_to_all(leaving, 'light', 0, 0, axis_index_groups=along)  15.7 us
    all_to_all x1, blocking collectives, local(): entering = lax.all_to_all(entering, 'light', 0, 0, axis_index_groups=along)  11.2 us
    all_gather x1, blocking collectives, local(): both = lax.all_gather(send, 'view', axis_index_groups=chips)  6.91 us
    pallas_call x1, Pallas kernels, local(): call(lambda *refs: brick_kernel(light_scale, view_scale, *refs), 'brick',...  2.44 us
    all_gather x1, blocking collectives, local(): both = lax.all_gather(send, 'view', axis_index_groups=cores)  2.28 us
    pallas_call x1, Pallas kernels, local(): call(lambda *refs: exit_kernel(light_scale, *refs), 'exits', lines, [pl.B...  1.88 us

profile of v4, /device:TPU:8, one launch (start us, length us, event | category | flops | bytes accessed | tf_op | source)
XLA Modules:
  0.0 65.3 jit_solution(12236766437523988228)
XLA Ops:
  0.0 0.0 copy-start.1
  0.0 1.9 %exits.1 = f32[16,24,128]{2,1,0:T(8,128)S(1)} custom-call(f32[8,8,2048]{2,1,0:T(8,128)} %refs_3_.1), custom_call_target="tpu_custom_call" | custom-call | tf_op jit(solution)/shard_map/exits/pallas_call | solution.py:243
  1.9 0.0 copy-start
  1.9 15.7 %all_to_all.15.refs_0_ = f32[16,24,128]{2,1,0:T(8,128)S(1)} all-to-all(f32[16,24,128]{2,1,0:T(8,128)S(1)} %exits.1), channel_id=1, replica_groups={{320,352,384,416,448,480,0,32,64,96,128,160,192,224,256,288},{321,353,3..., dimensions={0} | all-to-all | bytes 393216 | tf_op jit(solution)/shard_map/all_to_all | solution.py:255
  17.7 0.0 copy-start.3
  17.7 11.2 %all_to_all.16.refs_5_ = f32[16,24,128]{2,1,0:T(8,128)S(1)} all-to-all(f32[16,24,128]{2,1,0:T(8,128)S(1)} %prefix.1), channel_id=1, replica_groups={{320,352,384,416,448,480,0,32,64,96,128,160,192,224,256,288},{321,353,3..., dimensions={0} | all-to-all | bytes 393216 | tf_op jit(solution)/shard_map/all_to_all | solution.py:257
  28.9 0.0 copy-start.2
  28.9 0.0 copy-start.4
  28.9 0.0 copy-done.1
  28.9 0.0 copy-done
  28.9 0.0 copy-done.3
  28.9 0.6 copy-done.2
  29.6 0.0 copy-done.4
  29.6 2.4 %brick.1 = (f32[2,8,40,128]{3,2,1,0:T(8,128)S(1)}, f32[2,8,40,128]{3,2,1,0:T(8,128)S(1)}) custom-call(s32[8]{0:T(128)S(1)} %copy-done.2, s32[8]{0:T(128)S(1)} %copy-done.4, f32[3,8]{1,0:T(4,128)S(1)} %bitcast.5, f32[8,8,2048]{2,1,0:T(8,128)S(1)} %copy-done, bf16[3,8,8,2048]{3,2,1,0:T(8,128)(2,1)S(1)} %copy-done.1, f32[16,24,128]{2,1,0:T(8,128)S(1)} %all_to_all.16.refs_5_), custom_call_target="tpu_custom_call" | custom-call | tf_op jit(solution)/shard_map/brick/pallas_call | solution.py:259
  32.0 2.3 %all-gather = f32[4,8,40,128]{3,2,1,0:T(8,128)S(1)} all-gather(f32[2,8,40,128]{3,2,1,0:T(8,128)S(1)} %get-tuple-element.10), channel_id=2, replica_groups={{0,1},{2,3},{4,5},{6,7},{8,9},{10,11},{12,13},{14,15},{16,17},{18,19},{..., dimensions={0}, use_global_device_ids=true | all-gather | bytes 983040 | tf_op jit(solution)/shard_map/all_gather | solution.py:267
  34.3 0.6 cores.1
  34.9 6.9 %all-gather.1 = f32[16,40,128]{2,1,0:T(8,128)S(1)} all-gather(f32[8,40,128]{2,1,0:T(8,128)S(1)} %get-tuple-element.12), channel_id=3, replica_groups={{0,2},{1,3},{4,6},{5,7},{8,10},{9,11},{12,14},{13,15},{16,18},{17,19},{..., dimensions={0}, use_global_device_ids=true | all-gather | bytes 491520 | tf_op jit(solution)/shard_map/all_gather | solution.py:271
  41.8 0.6 chips.1
  42.4 21.6 %all_to_all.17.refs_3_ = f32[8,40,128]{2,1,0:T(8,128)S(1)} all-to-all(f32[8,40,128]{2,1,0:T(8,128)S(1)} %chips.1), channel_id=1, replica_groups={{20,24,28,0,4,8,12,16},{21,25,29,1,5,9,13,17},{22,26,30,2,6,10,14,18},{..., dimensions={0} | all-to-all | bytes 327680 | tf_op jit(solution)/shard_map/all_to_all | solution.py:274
  64.0 1.3 %final.1 = f32[8,4,512]{2,1,0:T(4,128)} custom-call(s32[8]{0:T(128)S(1)} %copy-done.2, s32[8]{0:T(128)S(1)} %copy-done.4, f32[3,8]{1,0:T(4,128)S(1)} %bitcast.6, f32[8,40,128]{2,1,0:T(8,128)S(1)} %all_to_all.17.refs_3_), custom_call_target="tpu_custom_call" | custom-call | tf_op jit(solution)/shard_map/final/pallas_call | solution.py:275
  (1 shorter events, 0.0 us)
Async XLA Ops:
  0.0 28.9 %copy-start.1 = (bf16[3,8,8,2048]{3,2,1,0:T(8,128)(2,1)S(1)}, bf16[3,8,8,2048]{3,2,1,0:T(8,128)(2,1)}, u32[]{:S(2)}) copy-start(bf16[3,8,8,2048]{3,2,1,0:T(8,128)(2,1)} %refs_4_.1) | copy-start | bytes 2359300
  1.9 27.0 %copy-start = (f32[8,8,2048]{2,1,0:T(8,128)S(1)}, f32[8,8,2048]{2,1,0:T(8,128)}, u32[]{:S(2)}) copy-start(f32[8,8,2048]{2,1,0:T(8,128)} %refs_3_.1) | copy-start | bytes 1572868
  17.7 11.2 %copy-start.3 = (f32[8,3]{0,1:T(4,128)S(1)}, f32[8,3]{0,1:T(4,128)}, u32[]{:S(2)}) copy-start(f32[8,3]{0,1:T(4,128)} %param.7) | copy-start | bytes 292
  28.9 0.7 %copy-start.2 = (s32[8]{0:T(128)S(1)}, s32[8]{0:T(128)}, u32[]{:S(2)}) copy-start(s32[8]{0:T(128)} %refs_0_.5) | copy-start | bytes 100
  28.9 0.7 %copy-start.4 = (s32[8]{0:T(128)S(1)}, s32[8]{0:T(128)}, u32[]{:S(2)}) copy-start(s32[8]{0:T(128)} %refs_1_.3) | copy-start | bytes 100

commit v5 on v4

--- a/solution.py
+++ b/solution.py
@@ -10,9 +10,11 @@
 VIEW_DEPTH = 2.0
 LANES = 128
 STEPS = (-1, 0, 1)
+CHANNELS = ((0, 0), (0, 1), (1, 0), (1, 1), (2, 0), (2, 1), (0, 2), (1, 2), (2, 2))
 ROWS = 40
-LIGHT_FIRST = 10
-VIEW_FIRST = 5
+LIGHT_ORDER = (10, 9, 8, 7, 6, 5, 4, 3, 2, 1, 0, 15, 14, 13, 12, 11)
+VIEW_ORDER = (5, 1, 3, 7, 4, 0, 2, 6)
+PARTS = 2
 
 
 def slide(planes, amount):
@@ -40,17 +42,24 @@
 def exit_kernel(scale, density_ref, exit_ref, dense_ref, total_ref, arrived):
     slices, cells, columns = density_ref.shape
     count = exit_ref.shape[0]
-    copies = [pltpu.make_async_copy(density_ref.at[k], dense_ref.at[k], arrived.at[k]) for k in range(slices)]
-    for copy in copies:
-        copy.start()
+    size = slices // PARTS
+    copies = []
+    for part in range(PARTS):
+        span = pl.ds(part * size, size)
+        copies.append(pltpu.make_async_copy(density_ref.at[span], dense_ref.at[span], arrived.at[part]))
+        copies[-1].start()
     amount = slices * (count - 1 - lax.axis_index("light"))
-    for k in range(slices):
-        copies[k].wait()
-        dense = dense_ref[k] * scale
+    for part, copy in enumerate(copies):
+        copy.wait()
         for index, step in enumerate(STEPS):
-            total_ref[index] = slide(total_ref[index] + dense if k else dense, step)
+            sums = [dense_ref[k] * scale for k in range(part * size, part * size + size)]
+            reach = 1
+            while len(sums) > 1:
+                sums = [slide(a, reach * step) + b for a, b in zip(sums[::2], sums[1::2])]
+                reach *= 2
+            total_ref[index] = slide(total_ref[index], size * step) + sums[0] if part else sums[0]
     for index, step in enumerate(STEPS):
-        total = total_ref[index]
+        total = slide(total_ref[index], step)
         groups = [total[:, g * LANES : (g + 1) * LANES] for g in range(count)]
         if step:
             groups = turn(groups, amount, step > 0)
@@ -58,17 +67,24 @@
             exit_ref[g, index * cells : (index + 1) * cells, :] = values
 
 
-def prefix_kernel(slices, leaving_ref, entering_ref):
+def spread(ref, row, column):
+    return jnp.broadcast_to(ref[row : row + 1, column : column + 1], (8, LANES))
+
+
+def prefix_kernel(slices, leaving_ref, flip_ref, shift_ref, color_ref, entering_ref, flips_ref):
+    for k in range(slices):
+        flips_ref[k] = spread(flip_ref, 0, k)
     count, planes, _ = leaving_ref.shape
     cells = planes // len(STEPS)
     columns = count * LANES
-    position = lax.rem(lax.axis_index("light") + count - LIGHT_FIRST, count)
+    light = lax.axis_index("light")
+    position = sum(jnp.where(light == member, p, 0) for p, member in enumerate(LIGHT_ORDER))
     place = position * LANES + lax.broadcasted_iota(jnp.int32, (cells, LANES), 1)
     for index, step in enumerate(STEPS):
         part = slice(index * cells, (index + 1) * cells)
         total = jnp.zeros((cells, LANES), jnp.float32)
         for j in range(count):
-            member = (j - LIGHT_FIRST) % count
+            member = LIGHT_ORDER.index(j)
             entering_ref[member, part, :] = total
             if step and j:
                 column = (place - step * slices * (count - 1 - j) + columns) & (columns - 1)
@@ -88,7 +104,7 @@
 
 
 def brick_kernel(
-    light_scale, view_scale, flip_ref, shift_ref, color_ref, density_ref, albedo_ref, entering_ref, keep_ref, send_ref, depth_ref, lit_ref
+    light_scale, view_scale, flips_ref, density_ref, albedo_ref, entering_ref, keep_ref, send_ref, depth_ref, lit_ref
 ):
     slices, cells, columns = density_ref.shape
     count = entering_ref.shape[0]
@@ -108,7 +124,7 @@
 
     def one_slice(k, carry):
         dense = density_ref[k]
-        flipped = flip_ref[k] == 1
+        flipped = jnp.concatenate([flips_ref[k]] * (columns // LANES), axis=1) == 1
         depth_view = dense * view_scale
         running = depth_view
         for reach in (1, 2, 4):
@@ -126,11 +142,10 @@
             for chunk in (2 * pair, 2 * pair + 1):
                 groups = [slice((4 * chunk + g) * LANES, (4 * chunk + g + 1) * LANES) for g in range(4)]
                 reflect = [[albedo_ref[c, k, :, g].astype(jnp.float32) for g in groups] for c in range(3)]
+                lit = [[lit_ref[index, :, g] for g in groups] for index in range(len(STEPS))]
                 products = []
-                for index in range(len(STEPS)):
-                    lit = [lit_ref[index, :, g] for g in groups]
-                    for c in range(3):
-                        products += [reflect[c][g] * lit[g] for g in range(4)]
+                for index, c in CHANNELS:
+                    products += [reflect[c][g] * lit[index][g] for g in range(4)]
                 products += [depth_view[:, g] for g in groups]
                 tiles = [gather_sums(products[t : t + 8], low) for t in range(0, ROWS, 8)]
                 tiles[-1] = jnp.where(low[2], tiles[-1], jnp.exp(jnp.where(low[2], 0.0, tiles[-1])))
@@ -170,50 +185,52 @@
     return composite([front, back], low)
 
 
-def core_kernel(flip_ref, keep_ref, both_ref, mine_ref, send_ref):
+def core_kernel(flips_ref, keep_ref, both_ref, mine_ref, send_ref):
     low = lax.broadcasted_iota(jnp.int32, (8, LANES), 0) < 4
     view = lax.axis_index("view")
     core, chip = view & 1, (view >> 1) & 1
     for k in range(keep_ref.shape[1]):
-        mine_front = core == flip_ref[k]
+        mine_front = flips_ref[k] == core
         for half, out_ref in ((chip, mine_ref), (1 - chip, send_ref)):
             merged = merge(tiles_of(keep_ref, half, k), tiles_of(both_ref, 1 - core, half, k), mine_front, low)
             for t, tile in enumerate(merged):
                 out_ref[k, 8 * t : 8 * t + 8, :] = tile
 
 
-def chip_kernel(flip_ref, mine_ref, both_ref, out_ref):
+def chip_kernel(flips_ref, mine_ref, both_ref, out_ref):
     low = lax.broadcasted_iota(jnp.int32, (8, LANES), 0) < 4
     chip = (lax.axis_index("view") >> 1) & 1
     for k in range(mine_ref.shape[0]):
-        merged = merge(tiles_of(mine_ref, k), tiles_of(both_ref, 1 - chip, k), chip == flip_ref[k], low)
+        merged = merge(tiles_of(mine_ref, k), tiles_of(both_ref, 1 - chip, k), flips_ref[k] == chip, low)
         for t, tile in enumerate(merged):
-            out_ref[(k - VIEW_FIRST) % mine_ref.shape[0], 8 * t : 8 * t + 8, :] = tile
-
-
-def final_kernel(per_slice, flip_ref, shift_ref, color_ref, pieces_ref, out_ref, sums_ref):
+            out_ref[VIEW_ORDER.index(k), 8 * t : 8 * t + 8, :] = tile
+
+
+def final_kernel(per_slice, flips_ref, shift_ref, color_ref, pieces_ref, out_ref, rows_ref):
     low = lax.broadcasted_iota(jnp.int32, (8, LANES), 0) < 4
     count = pieces_ref.shape[0]
-    flipped = flip_ref[lax.axis_index("view") // per_slice] == 1
-    order = [jnp.where(flipped, (count - 1 - j - VIEW_FIRST) % count, (j - VIEW_FIRST) % count) for j in range(count)]
-    for t, tile in enumerate(composite([tiles_of(pieces_ref, j) for j in order], low)):
-        sums_ref[8 * t : 8 * t + 8, :] = tile
+    flipped = flips_ref[lax.axis_index("view") // per_slice] == 1
+    ordered = []
+    for j in range(count):
+        near, far = tiles_of(pieces_ref, VIEW_ORDER.index(j)), tiles_of(pieces_ref, VIEW_ORDER.index(count - 1 - j))
+        ordered.append([jnp.where(flipped, b, a) for a, b in zip(near, far)])
+    first, second, third, blue, last = composite(ordered, low)
+    blue_second = pltpu.roll(blue, 4, axis=0)
+    opacity = 1.0 - last
     for light in range(LIGHTS):
-        base = (shift_ref[light] + 1) * 12
-        for c in range(3):
-            tint = color_ref[c, light]
-            for g in range(4):
-                out_ref[light, c : c + 1, g * LANES : (g + 1) * LANES] = sums_ref[pl.ds(base + 4 * c + g, 1), :] * tint
+        step = spread(shift_ref, 0, light)
+        red_green = jnp.where(step == 0, second, jnp.where(step < 0, first, third))
+        blues = jnp.where(step == 0, blue_second, jnp.where(step < 0, blue, last))
+        tint = [spread(color_ref, c, light) for c in range(3)]
+        rows_ref[light, 0:8, :] = red_green * jnp.where(low, tint[0], tint[1])
+        rows_ref[light, 8:16, :] = jnp.where(low, blues * tint[2], opacity)
+    for light in range(LIGHTS):
         for g in range(4):
-            out_ref[light, 3:4, g * LANES : (g + 1) * LANES] = 1.0 - sums_ref[36 + g : 37 + g, :]
+            out_ref[light, :, g * LANES : (g + 1) * LANES] = rows_ref[light, pl.ds(g, 4, stride=4), :]
 
 
 def vmem(count):
     return [pl.BlockSpec(memory_space=pltpu.VMEM)] * count
-
-
-def smem(count):
-    return [pl.BlockSpec(memory_space=pltpu.SMEM)] * count
 
 
 def local(density, albedo, light_color, light_shift, view_flip):
@@ -236,8 +253,8 @@
             compiler_params=pltpu.CompilerParams(vmem_limit_bytes=16 * 2**20),
         )
 
-    def shaped(*shape):
-        return jax.ShapeDtypeStruct(shape, f32)
+    def shaped(*shape, kind=f32):
+        return jax.ShapeDtypeStruct(shape, kind)
 
     lines = shaped(light_count, planes, columns // light_count)
     leaving = call(
@@ -248,37 +265,40 @@
         [
             pltpu.VMEM(density.shape, f32),
             pltpu.VMEM((len(STEPS), cells, columns), f32),
-            pltpu.SemaphoreType.DMA((slices,)),
+            pltpu.SemaphoreType.DMA((PARTS,)),
         ],
     )(pltpu.with_memory_space_constraint(density, pltpu.HBM))
-    along = [[(j + LIGHT_FIRST) % light_count for j in range(light_count)]]
+    leaving, albedo = lax.optimization_barrier((leaving, albedo))
+    along = [list(LIGHT_ORDER)]
     leaving = lax.all_to_all(leaving, "light", 0, 0, axis_index_groups=along)
-    entering = call(lambda *refs: prefix_kernel(slices, *refs), "prefix", lines, vmem(1))(leaving)
+    flip, shift, color = view_flip.reshape(1, -1), light_shift.reshape(1, -1), light_color.T
+    entering, flips = call(
+        lambda *refs: prefix_kernel(slices, *refs), "prefix", [lines, shaped(slices, 8, LANES, kind=jnp.int32)], vmem(4)
+    )(leaving, flip, shift, color)
     entering = lax.all_to_all(entering, "light", 0, 0, axis_index_groups=along)
-    color = light_color.T
     keep, send = call(
         lambda *refs: brick_kernel(light_scale, view_scale, *refs),
         "brick",
         [shaped(2, slices, ROWS, LANES)] * 2,
-        smem(3) + vmem(3),
+        vmem(4),
         [pltpu.VMEM((len(STEPS), cells, columns), f32), pltpu.VMEM((len(STEPS), cells, columns), f32)],
-    )(view_flip, light_shift, color, density, albedo, entering)
+    )(flips, density, albedo, entering)
     cores = [[2 * z, 2 * z + 1] for z in range(view_count // 2)]
     both = lax.all_gather(send, "view", axis_index_groups=cores)
     half = shaped(slices, ROWS, LANES)
-    mine, send = call(core_kernel, "cores", [half] * 2, smem(1) + vmem(2))(view_flip, keep, both)
+    mine, send = call(core_kernel, "cores", [half] * 2, vmem(3))(flips, keep, both)
     chips = [[v, v + 2] for v in range(view_count) if v & 2 == 0]
     both = lax.all_gather(send, "view", axis_index_groups=chips)
-    merged = call(chip_kernel, "chips", half, smem(1) + vmem(2))(view_flip, mine, both)
-    rest = [[4 * ((k + VIEW_FIRST) % slices) + r for k in range(slices)] for r in range(4)]
+    merged = call(chip_kernel, "chips", half, vmem(3))(flips, mine, both)
+    rest = [[4 * k + r for k in VIEW_ORDER] for r in range(4)]
     pieces = lax.all_to_all(merged, "view", 0, 0, axis_index_groups=rest)
     return call(
         lambda *refs: final_kernel(view_count // slices, *refs),
         "final",
         shaped(LIGHTS, 4, slices * columns // view_count),
-        smem(3) + vmem(1),
-        [pltpu.VMEM((ROWS, LANES), f32)],
-    )(view_flip, light_shift, color, pieces)
+        vmem(4),
+        [pltpu.VMEM((LIGHTS, 16, LANES), f32)],
+    )(flips, shift, color, pieces)
 
 
 def solution(mesh):

time: 65.6 us -> 61.8 us (0.942)
  Pallas kernels: 6.86 us -> 4.38 us
  blocking collectives: 57.7 us -> 56.7 us
    pallas_call x3, Pallas kernels: 1.25 us -> 0.19 us  [the longest x1 0.08 us: local(): call(lambda *refs: prefix_kernel(slices, *refs), 'prefix', [lines, shaped...]
    all_to_all x1, blocking collectives: 21.6 us -> 20.7 us  [local(): pieces = lax.all_to_all(merged, 'view', 0, 0, axis_index_groups=rest)]
where the time goes in v5:
time: 61.8 us; the launch traced here: 61.2 us
  blocking collectives  56.7 us (92%)
  Pallas kernels  4.38 us (7%)
    all_to_all x1, blocking collectives, local(): pieces = lax.all_to_all(merged, 'view', 0, 0, axis_index_groups=rest)  20.7 us
    all_to_all x1, blocking collectives, local(): leaving = lax.all_to_all(leaving, 'light', 0, 0, axis_index_groups=along)  15.7 us
    all_to_all x1, blocking collectives, local(): entering = lax.all_to_all(entering, 'light', 0, 0, axis_index_groups=along)  11.1 us
    all_gather x1, blocking collectives, local(): both = lax.all_gather(send, 'view', axis_index_groups=chips)  6.91 us
    all_gather x1, blocking collectives, local(): both = lax.all_gather(send, 'view', axis_index_groups=cores)  2.28 us
    pallas_call x1, Pallas kernels, local(): call(lambda *refs: brick_kernel(light_scale, view_scale, *refs), 'brick',...  1.83 us
    pallas_call x1, Pallas kernels, local(): call(lambda *refs: exit_kernel(light_scale, *refs), 'exits', lines, [pl.B...  1.61 us

profile of v5, /device:TPU:8, one launch (start us, length us, event | category | flops | bytes accessed | tf_op | source)
XLA Modules:
  0.0 61.2 jit_solution(10012051541094419091)
XLA Ops:
  0.0 0.0 copy-start.1
  0.0 0.0 copy-start.2
  0.0 0.0 copy-start.3
  0.0 0.0 copy-start.4
  0.0 1.6 %exits.1 = f32[16,24,128]{2,1,0:T(8,128)S(1)} custom-call(f32[8,8,2048]{2,1,0:T(8,128)} %refs_1_.1), custom_call_target="tpu_custom_call" | custom-call | tf_op jit(solution)/shard_map/exits/pallas_call | solution.py:260
  1.6 0.0 copy-start
  1.6 15.7 %all_to_all.15.refs_0_ = f32[16,24,128]{2,1,0:T(8,128)S(1)} all-to-all(f32[16,24,128]{2,1,0:T(8,128)S(1)} %exits.1), channel_id=1, replica_groups={{320,288,256,224,192,160,128,96,64,32,0,480,448,416,384,352},{321,289,2..., dimensions={0} | all-to-all | bytes 393216 | tf_op jit(solution)/shard_map/all_to_all | solution.py:273
  17.4 0.0 copy-done.2
  17.4 0.0 copy-done.3
  17.4 0.0 copy-done.4
  17.4 0.1 prefix.1
  17.5 11.1 %all_to_all.16.refs_3_ = f32[16,24,128]{2,1,0:T(8,128)S(1)} all-to-all(f32[16,24,128]{2,1,0:T(8,128)S(1)} %get-tuple-element.16), channel_id=1, replica_groups={{320,288,256,224,192,160,128,96,64,32,0,480,448,416,384,352},{321,289,2..., dimensions={0} | all-to-all | bytes 393216 | tf_op jit(solution)/shard_map/all_to_all | solution.py:278
  28.5 0.0 copy-done.1
  28.5 0.0 copy-done
  28.5 1.8 %brick.1 = (f32[2,8,40,128]{3,2,1,0:T(8,128)S(1)}, f32[2,8,40,128]{3,2,1,0:T(8,128)S(1)}) custom-call(s32[8,8,128]{2,1,0:T(8,128)S(1)} %get-tuple-element.14.refs_0_.flips_ref, f32[8,8,2048]{2,1,0:T(8,128)S(1)} %copy-done, bf16[3,8,8,2048]{3,2,1,0:T(8,128)(2,1)S(1)} %copy-done.1, f32[16,24,128]{2,1,0:T(8,128)S(1)} %all_to_all.16.refs_3_), custom_call_target="tpu_custom_call" | custom-call | tf_op jit(solution)/shard_map/brick/pallas_call | solution.py:279
  30.4 2.3 %all-gather = f32[4,8,40,128]{3,2,1,0:T(8,128)S(1)} all-gather(f32[2,8,40,128]{3,2,1,0:T(8,128)S(1)} %get-tuple-element.18), channel_id=2, replica_groups={{0,1},{2,3},{4,5},{6,7},{8,9},{10,11},{12,13},{14,15},{16,17},{18,19},{..., dimensions={0}, use_global_device_ids=true | all-gather | bytes 983040 | tf_op jit(solution)/shard_map/all_gather | solution.py:287
  32.7 0.1 cores.1
  32.7 6.9 %all-gather.1 = f32[16,40,128]{2,1,0:T(8,128)S(1)} all-gather(f32[8,40,128]{2,1,0:T(8,128)S(1)} %get-tuple-element.20), channel_id=3, replica_groups={{0,2},{1,3},{4,6},{5,7},{8,10},{9,11},{12,14},{13,15},{16,18},{17,19},{..., dimensions={0}, use_global_device_ids=true | all-gather | bytes 491520 | tf_op jit(solution)/shard_map/all_gather | solution.py:291
  39.7 20.7 %all_to_all.17.refs_3_ = f32[8,40,128]{2,1,0:T(8,128)S(1)} all-to-all(f32[8,40,128]{2,1,0:T(8,128)S(1)} %chips.1), channel_id=1, replica_groups={{20,4,12,28,16,0,8,24},{21,5,13,29,17,1,9,25},{22,6,14,30,18,2,10,26},{..., dimensions={0} | all-to-all | bytes 327680 | tf_op jit(solution)/shard_map/all_to_all | solution.py:294
  60.4 0.8 %final.1 = f32[8,4,512]{2,1,0:T(4,128)} custom-call(s32[8,8,128]{2,1,0:T(8,128)S(1)} %get-tuple-element.14.refs_0_.flips_ref, s32[1,8]{1,0:T(1,128)S(1)} %bitcast.10, f32[3,8]{1,0:T(4,128)S(1)} %bitcast.8, f32[8,40,128]{2,1,0:T(8,128)S(1)} %all_to_all.17.refs_3_), custom_call_target="tpu_custom_call" | custom-call | tf_op jit(solution)/shard_map/final/pallas_call | solution.py:295
  (1 shorter events, 0.0 us)
Async XLA Ops:
  0.0 28.5 %copy-start.1 = (bf16[3,8,8,2048]{3,2,1,0:T(8,128)(2,1)S(1)}, bf16[3,8,8,2048]{3,2,1,0:T(8,128)(2,1)}, u32[]{:S(2)}) copy-start(bf16[3,8,8,2048]{3,2,1,0:T(8,128)(2,1)} %refs_2_) | copy-start | bytes 2359300
  0.0 17.4 %copy-start.2 = (f32[8,3]{0,1:T(4,128)S(1)}, f32[8,3]{0,1:T(4,128)}, u32[]{:S(2)}) copy-start(f32[8,3]{0,1:T(4,128)} %param.7) | copy-start | bytes 292
  0.0 17.4 %copy-start.3 = (s32[8]{0:T(128)S(1)}, s32[8]{0:T(128)}, u32[]{:S(2)}) copy-start(s32[8]{0:T(128)} %param.8) | copy-start | bytes 100
  0.0 17.4 %copy-start.4 = (s32[8]{0:T(128)S(1)}, s32[8]{0:T(128)}, u32[]{:S(2)}) copy-start(s32[8]{0:T(128)} %param.9) | copy-start | bytes 100
  1.6 26.9 %copy-start = (f32[8,8,2048]{2,1,0:T(8,128)S(1)}, f32[8,8,2048]{2,1,0:T(8,128)}, u32[]{:S(2)}) copy-start(f32[8,8,2048]{2,1,0:T(8,128)} %refs_1_.1) | copy-start | bytes 1572868

commit v6 on v5

--- a/solution.py
+++ b/solution.py
@@ -1,3 +1,5 @@
+import math
+
 import jax
 import jax.numpy as jnp
 from jax import lax
@@ -13,7 +15,7 @@
 CHANNELS = ((0, 0), (0, 1), (1, 0), (1, 1), (2, 0), (2, 1), (0, 2), (1, 2), (2, 2))
 ROWS = 40
 LIGHT_ORDER = (10, 9, 8, 7, 6, 5, 4, 3, 2, 1, 0, 15, 14, 13, 12, 11)
-VIEW_ORDER = (5, 1, 3, 7, 4, 0, 2, 6)
+VIEW_ORDER = (5, 1, 3, 7, 0, 4, 2, 6)
 PARTS = 2
 
 
@@ -93,18 +95,17 @@
             total = total + leaving_ref[member, part, :]
 
 
-def gather_sums(parts, low):
-    for bit, mask in enumerate(low):
-        merged = []
-        for i in range(0, len(parts), 2):
-            a, b = parts[i], parts[i + 1]
-            merged.append(jnp.where(mask, a, b) + pltpu.roll(jnp.where(mask, b, a), 1 << bit, axis=0))
-        parts = merged
-    return parts[0]
+def gather_sums(parts, ref, base):
+    for r, part in enumerate(parts):
+        ref[base + 8 * r : base + 8 * r + 8, :] = part
+    rows = [ref[pl.ds(base + y, 8, stride=8), :] for y in range(8)]
+    while len(rows) > 1:
+        rows = [a + b for a, b in zip(rows[::2], rows[1::2])]
+    return rows[0]
 
 
 def brick_kernel(
-    light_scale, view_scale, flips_ref, density_ref, albedo_ref, entering_ref, keep_ref, send_ref, depth_ref, lit_ref
+    light_scale, view_scale, flips_ref, density_ref, albedo_ref, entering_ref, keep_ref, send_ref, depth_ref, lit_ref, turn_ref
 ):
     slices, cells, columns = density_ref.shape
     count = entering_ref.shape[0]
@@ -117,8 +118,7 @@
         for g, values in enumerate(groups):
             depth_ref[index, :, g * LANES : (g + 1) * LANES] = values
 
-    row = lax.broadcasted_iota(jnp.int32, (cells, LANES), 0)
-    low = [(row & (1 << bit)) == 0 for bit in range(3)]
+    low = lax.broadcasted_iota(jnp.int32, (cells, LANES), 0) < 4
     row_wide = lax.broadcasted_iota(jnp.int32, (cells, columns), 0)
     mine_even = core == 0
 
@@ -131,11 +131,11 @@
             running = running + jnp.where(row_wide >= reach, pltpu.roll(running, reach, axis=0), 0.0)
         total = jnp.broadcast_to(running[cells - 1 :, :], (cells, columns))
         ahead = jnp.where(flipped, total - running, running - depth_view)
-        weights = jnp.exp(ahead) * (1.0 - jnp.exp(depth_view))
+        weights = jnp.exp2(ahead) * (1.0 - jnp.exp2(depth_view))
         dense_light = dense * light_scale
         for index, step in enumerate(STEPS):
             depth = depth_ref[index]
-            lit_ref[index] = weights * jnp.exp(depth)
+            lit_ref[index] = weights * jnp.exp2(depth)
             depth_ref[index] = slide(depth + dense_light, step)
         for pair in range(columns // (8 * LANES)):
             chunks = []
@@ -147,15 +147,15 @@
                 for index, c in CHANNELS:
                     products += [reflect[c][g] * lit[index][g] for g in range(4)]
                 products += [depth_view[:, g] for g in groups]
-                tiles = [gather_sums(products[t : t + 8], low) for t in range(0, ROWS, 8)]
-                tiles[-1] = jnp.where(low[2], tiles[-1], jnp.exp(jnp.where(low[2], 0.0, tiles[-1])))
+                tiles = [gather_sums(products[t : t + 8], turn_ref, 8 * (chunk * ROWS + t)) for t in range(0, ROWS, 8)]
+                tiles[-1] = jnp.where(low, tiles[-1], jnp.exp2(jnp.where(low, 0.0, tiles[-1])))
                 chunks.append(tiles)
             for t, (even, odd) in enumerate(zip(*chunks)):
                 keep_ref[pair, k, 8 * t : 8 * t + 8, :] = jnp.where(mine_even, even, odd)
                 send_ref[pair, k, 8 * t : 8 * t + 8, :] = jnp.where(mine_even, odd, even)
         return carry
 
-    lax.fori_loop(0, slices, one_slice, 0)
+    lax.fori_loop(0, slices, one_slice, 0, unroll=2)
 
 
 def both_halves(tile, low):
@@ -236,8 +236,8 @@
 def local(density, albedo, light_color, light_shift, view_flip):
     slices, cells, columns = density.shape
     light_count, view_count = lax.axis_size("light"), lax.axis_size("view")
-    light_scale = -LIGHT_DEPTH / (slices * light_count)
-    view_scale = -VIEW_DEPTH / (cells * view_count)
+    light_scale = -LIGHT_DEPTH / (slices * light_count) * math.log2(math.e)
+    view_scale = -VIEW_DEPTH / (cells * view_count) * math.log2(math.e)
     planes = len(STEPS) * cells
     f32 = jnp.float32
 
@@ -281,7 +281,11 @@
         "brick",
         [shaped(2, slices, ROWS, LANES)] * 2,
         vmem(4),
-        [pltpu.VMEM((len(STEPS), cells, columns), f32), pltpu.VMEM((len(STEPS), cells, columns), f32)],
+        [
+            pltpu.VMEM((len(STEPS), cells, columns), f32),
+            pltpu.VMEM((len(STEPS), cells, columns), f32),
+            pltpu.VMEM((columns // (4 * LANES) * ROWS * cells, LANES), f32),
+        ],
     )(flips, density, albedo, entering)
     cores = [[2 * z, 2 * z + 1] for z in range(view_count // 2)]
     both = lax.all_gather(send, "view", axis_index_groups=cores)

time: 61.8 us -> 61 us (0.987)
  no operation moved by 1% of the time
where the time goes in v6:
time: 61 us; the launch traced here: 60.8 us
  blocking collectives  56.5 us (93%)
  Pallas kernels  4.22 us (7%)
    all_to_all x1, blocking collectives, local(): pieces = lax.all_to_all(merged, 'view', 0, 0, axis_index_groups=rest)  20.5 us
    all_to_all x1, blocking collectives, local(): leaving = lax.all_to_all(leaving, 'light', 0, 0, axis_index_groups=along)  15.7 us
    all_to_all x1, blocking collectives, local(): entering = lax.all_to_all(entering, 'light', 0, 0, axis_index_groups=along)  11.1 us
    all_gather x1, blocking collectives, local(): both = lax.all_gather(send, 'view', axis_index_groups=chips)  6.91 us
    all_gather x1, blocking collectives, local(): both = lax.all_gather(send, 'view', axis_index_groups=cores)  2.28 us
    pallas_call x1, Pallas kernels, local(): call(lambda *refs: brick_kernel(light_scale, view_scale, *refs), 'brick',...  1.66 us
    pallas_call x1, Pallas kernels, local(): call(lambda *refs: exit_kernel(light_scale, *refs), 'exits', lines, [pl.B...  1.61 us

profile of v6, /device:TPU:8, one launch (start us, length us, event | category | flops | bytes accessed | tf_op | source)
XLA Modules:
  0.0 60.8 jit_solution(8000769009899571879)
XLA Ops:
  0.0 0.0 copy-start.1
  0.0 0.0 copy-start.2
  0.0 0.0 copy-start.3
  0.0 0.0 copy-start.4
  0.0 1.6 %exits.1 = f32[16,24,128]{2,1,0:T(8,128)S(1)} custom-call(f32[8,8,2048]{2,1,0:T(8,128)} %refs_1_.1), custom_call_target="tpu_custom_call" | custom-call | tf_op jit(solution)/shard_map/exits/pallas_call | solution.py:260
  1.6 0.0 copy-start
  1.6 15.7 %all_to_all.15.refs_0_ = f32[16,24,128]{2,1,0:T(8,128)S(1)} all-to-all(f32[16,24,128]{2,1,0:T(8,128)S(1)} %exits.1), channel_id=1, replica_groups={{320,288,256,224,192,160,128,96,64,32,0,480,448,416,384,352},{321,289,2..., dimensions={0} | all-to-all | bytes 393216 | tf_op jit(solution)/shard_map/all_to_all | solution.py:273
  17.4 0.0 copy-done.2
  17.4 0.0 copy-done.3
  17.4 0.0 copy-done.4
  17.4 0.1 prefix.1
  17.5 11.1 %all_to_all.16.refs_3_ = f32[16,24,128]{2,1,0:T(8,128)S(1)} all-to-all(f32[16,24,128]{2,1,0:T(8,128)S(1)} %get-tuple-element.16), channel_id=1, replica_groups={{320,288,256,224,192,160,128,96,64,32,0,480,448,416,384,352},{321,289,2..., dimensions={0} | all-to-all | bytes 393216 | tf_op jit(solution)/shard_map/all_to_all | solution.py:278
  28.5 0.0 copy-done.1
  28.5 0.0 copy-done
  28.5 1.7 %brick.1 = (f32[2,8,40,128]{3,2,1,0:T(8,128)S(1)}, f32[2,8,40,128]{3,2,1,0:T(8,128)S(1)}) custom-call(s32[8,8,128]{2,1,0:T(8,128)S(1)} %get-tuple-element.14.refs_0_.flips_ref, f32[8,8,2048]{2,1,0:T(8,128)S(1)} %copy-done, bf16[3,8,8,2048]{3,2,1,0:T(8,128)(2,1)S(1)} %copy-done.1, f32[16,24,128]{2,1,0:T(8,128)S(1)} %all_to_all.16.refs_3_), custom_call_target="tpu_custom_call" | custom-call | tf_op jit(solution)/shard_map/brick/pallas_call | solution.py:279
  30.2 2.3 %all-gather = f32[4,8,40,128]{3,2,1,0:T(8,128)S(1)} all-gather(f32[2,8,40,128]{3,2,1,0:T(8,128)S(1)} %get-tuple-element.18), channel_id=2, replica_groups={{0,1},{2,3},{4,5},{6,7},{8,9},{10,11},{12,13},{14,15},{16,17},{18,19},{..., dimensions={0}, use_global_device_ids=true | all-gather | bytes 983040 | tf_op jit(solution)/shard_map/all_gather | solution.py:291
  32.5 0.1 cores.1
  32.6 6.9 %all-gather.1 = f32[16,40,128]{2,1,0:T(8,128)S(1)} all-gather(f32[8,40,128]{2,1,0:T(8,128)S(1)} %get-tuple-element.20), channel_id=3, replica_groups={{0,2},{1,3},{4,6},{5,7},{8,10},{9,11},{12,14},{13,15},{16,18},{17,19},{..., dimensions={0}, use_global_device_ids=true | all-gather | bytes 491520 | tf_op jit(solution)/shard_map/all_gather | solution.py:295
  39.5 20.5 %all_to_all.17.refs_3_ = f32[8,40,128]{2,1,0:T(8,128)S(1)} all-to-all(f32[8,40,128]{2,1,0:T(8,128)S(1)} %chips.1), channel_id=1, replica_groups={{20,4,12,28,0,16,8,24},{21,5,13,29,1,17,9,25},{22,6,14,30,2,18,10,26},{..., dimensions={0} | all-to-all | bytes 327680 | tf_op jit(solution)/shard_map/all_to_all | solution.py:298
  60.0 0.8 %final.1 = f32[8,4,512]{2,1,0:T(4,128)} custom-call(s32[8,8,128]{2,1,0:T(8,128)S(1)} %get-tuple-element.14.refs_0_.flips_ref, s32[1,8]{1,0:T(1,128)S(1)} %bitcast.10, f32[3,8]{1,0:T(4,128)S(1)} %bitcast.8, f32[8,40,128]{2,1,0:T(8,128)S(1)} %all_to_all.17.refs_3_), custom_call_target="tpu_custom_call" | custom-call | tf_op jit(solution)/shard_map/final/pallas_call | solution.py:299
  (1 shorter events, 0.0 us)
Async XLA Ops:
  0.0 28.5 %copy-start.1 = (bf16[3,8,8,2048]{3,2,1,0:T(8,128)(2,1)S(1)}, bf16[3,8,8,2048]{3,2,1,0:T(8,128)(2,1)}, u32[]{:S(2)}) copy-start(bf16[3,8,8,2048]{3,2,1,0:T(8,128)(2,1)} %refs_2_) | copy-start | bytes 2359300
  0.0 17.4 %copy-start.2 = (f32[8,3]{0,1:T(4,128)S(1)}, f32[8,3]{0,1:T(4,128)}, u32[]{:S(2)}) copy-start(f32[8,3]{0,1:T(4,128)} %param.7) | copy-start | bytes 292
  0.0 17.4 %copy-start.3 = (s32[8]{0:T(128)S(1)}, s32[8]{0:T(128)}, u32[]{:S(2)}) copy-start(s32[8]{0:T(128)} %param.8) | copy-start | bytes 100
  0.0 17.4 %copy-start.4 = (s32[8]{0:T(128)S(1)}, s32[8]{0:T(128)}, u32[]{:S(2)}) copy-start(s32[8]{0:T(128)} %param.9) | copy-start | bytes 100
  1.6 26.9 %copy-start = (f32[8,8,2048]{2,1,0:T(8,128)S(1)}, f32[8,8,2048]{2,1,0:T(8,128)}, u32[]{:S(2)}) copy-start(f32[8,8,2048]{2,1,0:T(8,128)} %refs_1_.1) | copy-start | bytes 1572868

commit v7 on v6

--- a/solution.py
+++ b/solution.py
@@ -104,6 +104,17 @@
     return rows[0]
 
 
+def merged_rows(a, b, row, bit):
+    mask = (row & (1 << bit)) == 0
+    return jnp.where(mask, a, b) + pltpu.roll(jnp.where(mask, b, a), 1 << bit, axis=0)
+
+
+def last_tile(parts, totals, row):
+    sums = merged_rows(merged_rows(*parts[:2], row, 0), merged_rows(*parts[2:], row, 0), row, 1)
+    depth = jnp.where(row == 4, totals[0], jnp.where(row == 5, totals[1], jnp.where(row == 6, totals[2], totals[3])))
+    return jnp.where(row < 4, sums + pltpu.roll(sums, 4, axis=0), jnp.exp2(depth))
+
+
 def brick_kernel(
     light_scale, view_scale, flips_ref, density_ref, albedo_ref, entering_ref, keep_ref, send_ref, depth_ref, lit_ref, turn_ref
 ):
@@ -118,7 +129,7 @@
         for g, values in enumerate(groups):
             depth_ref[index, :, g * LANES : (g + 1) * LANES] = values
 
-    low = lax.broadcasted_iota(jnp.int32, (cells, LANES), 0) < 4
+    row = lax.broadcasted_iota(jnp.int32, (cells, LANES), 0)
     row_wide = lax.broadcasted_iota(jnp.int32, (cells, columns), 0)
     mine_even = core == 0
 
@@ -146,9 +157,8 @@
                 products = []
                 for index, c in CHANNELS:
                     products += [reflect[c][g] * lit[index][g] for g in range(4)]
-                products += [depth_view[:, g] for g in groups]
-                tiles = [gather_sums(products[t : t + 8], turn_ref, 8 * (chunk * ROWS + t)) for t in range(0, ROWS, 8)]
-                tiles[-1] = jnp.where(low, tiles[-1], jnp.exp2(jnp.where(low, 0.0, tiles[-1])))
+                tiles = [gather_sums(products[t : t + 8], turn_ref, 8 * (chunk * ROWS + t)) for t in range(0, ROWS - 8, 8)]
+                tiles.append(last_tile(products[ROWS - 8 :], [total[:, g] for g in groups], row))
                 chunks.append(tiles)
             for t, (even, odd) in enumerate(zip(*chunks)):
                 keep_ref[pair, k, 8 * t : 8 * t + 8, :] = jnp.where(mine_even, even, odd)

time: 61 us -> 61 us (level)
  no operation moved by 1% of the time
where the time goes in v7:
time: 61 us; the launch traced here: 60.8 us
  blocking collectives  56.5 us (93%)
  Pallas kernels  4.24 us (7%)
    all_to_all x1, blocking collectives, local(): pieces = lax.all_to_all(merged, 'view', 0, 0, axis_index_groups=rest)  20.5 us
    all_to_all x1, blocking collectives, local(): leaving = lax.all_to_all(leaving, 'light', 0, 0, axis_index_groups=along)  15.7 us
    all_to_all x1, blocking collectives, local(): entering = lax.all_to_all(entering, 'light', 0, 0, axis_index_groups=along)  11.1 us
    all_gather x1, blocking collectives, local(): both = lax.all_gather(send, 'view', axis_index_groups=chips)  6.91 us
    all_gather x1, blocking collectives, local(): both = lax.all_gather(send, 'view', axis_index_groups=cores)  2.28 us
    pallas_call x1, Pallas kernels, local(): call(lambda *refs: brick_kernel(light_scale, view_scale, *refs), 'brick',...  1.68 us
    pallas_call x1, Pallas kernels, local(): call(lambda *refs: exit_kernel(light_scale, *refs), 'exits', lines, [pl.B...  1.61 us

profile of v7, /device:TPU:8, one launch (start us, length us, event | category | flops | bytes accessed | tf_op | source)
XLA Modules:
  0.0 60.8 jit_solution(129676762485674096)
XLA Ops:
  0.0 0.0 copy-start.1
  0.0 0.0 copy-start.2
  0.0 0.0 copy-start.3
  0.0 0.0 copy-start.4
  0.0 1.6 %exits.1 = f32[16,24,128]{2,1,0:T(8,128)S(1)} custom-call(f32[8,8,2048]{2,1,0:T(8,128)} %refs_1_.1), custom_call_target="tpu_custom_call" | custom-call | tf_op jit(solution)/shard_map/exits/pallas_call | solution.py:270
  1.6 0.0 copy-start
  1.6 15.7 %all_to_all.15.refs_0_ = f32[16,24,128]{2,1,0:T(8,128)S(1)} all-to-all(f32[16,24,128]{2,1,0:T(8,128)S(1)} %exits.1), channel_id=1, replica_groups={{320,288,256,224,192,160,128,96,64,32,0,480,448,416,384,352},{321,289,2..., dimensions={0} | all-to-all | bytes 393216 | tf_op jit(solution)/shard_map/all_to_all | solution.py:283
  17.4 0.0 copy-done.2
  17.4 0.0 copy-done.3
  17.4 0.0 copy-done.4
  17.4 0.1 prefix.1
  17.5 11.1 %all_to_all.16.refs_3_ = f32[16,24,128]{2,1,0:T(8,128)S(1)} all-to-all(f32[16,24,128]{2,1,0:T(8,128)S(1)} %get-tuple-element.16), channel_id=1, replica_groups={{320,288,256,224,192,160,128,96,64,32,0,480,448,416,384,352},{321,289,2..., dimensions={0} | all-to-all | bytes 393216 | tf_op jit(solution)/shard_map/all_to_all | solution.py:288
  28.5 0.0 copy-done.1
  28.5 0.0 copy-done
  28.5 1.7 %brick.1 = (f32[2,8,40,128]{3,2,1,0:T(8,128)S(1)}, f32[2,8,40,128]{3,2,1,0:T(8,128)S(1)}) custom-call(s32[8,8,128]{2,1,0:T(8,128)S(1)} %get-tuple-element.14.refs_0_.flips_ref, f32[8,8,2048]{2,1,0:T(8,128)S(1)} %copy-done, bf16[3,8,8,2048]{3,2,1,0:T(8,128)(2,1)S(1)} %copy-done.1, f32[16,24,128]{2,1,0:T(8,128)S(1)} %all_to_all.16.refs_3_), custom_call_target="tpu_custom_call" | custom-call | tf_op jit(solution)/shard_map/brick/pallas_call | solution.py:289
  30.2 2.3 %all-gather = f32[4,8,40,128]{3,2,1,0:T(8,128)S(1)} all-gather(f32[2,8,40,128]{3,2,1,0:T(8,128)S(1)} %get-tuple-element.18), channel_id=2, replica_groups={{0,1},{2,3},{4,5},{6,7},{8,9},{10,11},{12,13},{14,15},{16,17},{18,19},{..., dimensions={0}, use_global_device_ids=true | all-gather | bytes 983040 | tf_op jit(solution)/shard_map/all_gather | solution.py:301
  32.5 0.1 cores.1
  32.6 6.9 %all-gather.1 = f32[16,40,128]{2,1,0:T(8,128)S(1)} all-gather(f32[8,40,128]{2,1,0:T(8,128)S(1)} %get-tuple-element.20), channel_id=3, replica_groups={{0,2},{1,3},{4,6},{5,7},{8,10},{9,11},{12,14},{13,15},{16,18},{17,19},{..., dimensions={0}, use_global_device_ids=true | all-gather | bytes 491520 | tf_op jit(solution)/shard_map/all_gather | solution.py:305
  39.5 20.5 %all_to_all.17.refs_3_ = f32[8,40,128]{2,1,0:T(8,128)S(1)} all-to-all(f32[8,40,128]{2,1,0:T(8,128)S(1)} %chips.1), channel_id=1, replica_groups={{20,4,12,28,0,16,8,24},{21,5,13,29,1,17,9,25},{22,6,14,30,2,18,10,26},{..., dimensions={0} | all-to-all | bytes 327680 | tf_op jit(solution)/shard_map/all_to_all | solution.py:308
  60.0 0.8 %final.1 = f32[8,4,512]{2,1,0:T(4,128)} custom-call(s32[8,8,128]{2,1,0:T(8,128)S(1)} %get-tuple-element.14.refs_0_.flips_ref, s32[1,8]{1,0:T(1,128)S(1)} %bitcast.10, f32[3,8]{1,0:T(4,128)S(1)} %bitcast.8, f32[8,40,128]{2,1,0:T(8,128)S(1)} %all_to_all.17.refs_3_), custom_call_target="tpu_custom_call" | custom-call | tf_op jit(solution)/shard_map/final/pallas_call | solution.py:309
  (1 shorter events, 0.0 us)
Async XLA Ops:
  0.0 28.5 %copy-start.1 = (bf16[3,8,8,2048]{3,2,1,0:T(8,128)(2,1)S(1)}, bf16[3,8,8,2048]{3,2,1,0:T(8,128)(2,1)}, u32[]{:S(2)}) copy-start(bf16[3,8,8,2048]{3,2,1,0:T(8,128)(2,1)} %refs_2_) | copy-start | bytes 2359300
  0.0 17.4 %copy-start.2 = (f32[8,3]{0,1:T(4,128)S(1)}, f32[8,3]{0,1:T(4,128)}, u32[]{:S(2)}) copy-start(f32[8,3]{0,1:T(4,128)} %param.7) | copy-start | bytes 292
  0.0 17.4 %copy-start.3 = (s32[8]{0:T(128)S(1)}, s32[8]{0:T(128)}, u32[]{:S(2)}) copy-start(s32[8]{0:T(128)} %param.8) | copy-start | bytes 100
  0.0 17.4 %copy-start.4 = (s32[8]{0:T(128)S(1)}, s32[8]{0:T(128)}, u32[]{:S(2)}) copy-start(s32[8]{0:T(128)} %param.9) | copy-start | bytes 100
  1.6 26.9 %copy-start = (f32[8,8,2048]{2,1,0:T(8,128)S(1)}, f32[8,8,2048]{2,1,0:T(8,128)}, u32[]{:S(2)}) copy-start(f32[8,8,2048]{2,1,0:T(8,128)} %refs_1_.1) | copy-start | bytes 1572868
